TPU v7x, 256 devices: a whole 4x4x8 slice. The times are simulated.
256 devices in a mesh: row: 2 (over core), col: 128 (over z, y, x).
Axes of the slice: x: 4, y: 4, z: 8, core: 2. Of those that a mesh axis runs over, the one named last changes fastest.
Arguments:
- image_tokens: bfloat16 [64, 4096, 256], P('row', 'col'), may hold values from -6 to 6
- w_in: bfloat16 [256, 768], replicated, may hold values from -0.375 to 0.375
- conv_kernel: bfloat16 [3, 3, 768], replicated, may hold values from -2 to 2
- conv_bias: float32 [768], replicated, may hold values from -3 to 3
- long_filter: bfloat16 [64, 256], replicated, may hold values from -0.75 to 0.75
- skip_gain: float32 [256], replicated, may hold values from 0.5 to 1.5
- w_out: bfloat16 [256, 256], replicated, may hold values from -0.375 to 0.375
Outputs:
- layer_out: bfloat16 [64, 4096, 256], P('row', 'col')
All inputs are finite; a program needn't handle non-finite values.
Results may differ from a plain program's by a relative error of at most 0.014.
Values may be sent and summed in bfloat16 or wider, within the bound.
A program may use at most 64 MiB of HBM per device.

v0:
```python
import jax
import jax.numpy as jnp
from jax import lax
from jax.sharding import PartitionSpec as P


def extended(block, sides, width):
    for axis, dim in sides:
        count = lax.axis_size(axis)
        forward = [(i, i + 1) for i in range(count - 1)]
        backward = [(target, source) for source, target in forward]
        low = lax.ppermute(
            lax.slice_in_dim(block, block.shape[dim] - width, None, axis=dim), axis, forward
        )
        high = lax.ppermute(lax.slice_in_dim(block, 0, width, axis=dim), axis, backward)
        block = jnp.concatenate([low, block, high], axis=dim)
    return block


def depthwise(padded, kernel, bias, height, span):
    total = jnp.zeros((height, span, padded.shape[2]), jnp.float32) + bias
    for row_off in range(3):
        for col_off in range(3):
            window = padded[row_off : row_off + height, col_off : col_off + span, :].astype(
                jnp.float32
            )
            total = total + window * kernel[row_off, col_off].astype(jnp.float32)
    return total.astype(jnp.bfloat16)


def toeplitz(filt_rev, offset, out_count, src_count):
    margin = filt_rev.shape[0] // 3
    spare = margin // 2
    length = out_count + src_count - 1
    start = jnp.asarray(margin + margin - 1 - spare - (out_count - 1), jnp.int32) - jnp.asarray(
        offset, jnp.int32
    )
    window = lax.dynamic_slice_in_dim(filt_rev, start, length, 0)
    tiled = jnp.tile(window, (out_count + 1, 1))
    strided = tiled[out_count - 1 : out_count - 1 + out_count * (length - 1)]
    return strided.reshape(out_count, length - 1, filt_rev.shape[1])[:, :src_count]


def on_device(image_tokens, w_in, conv_kernel, conv_bias, long_filter, skip_gain, w_out):
    row_count, col_count, width = image_tokens.shape
    flat = image_tokens.reshape(row_count * col_count, width)
    projected = jnp.dot(flat, w_in, preferred_element_type=jnp.float32)
    projected = projected.astype(jnp.bfloat16).reshape(row_count, col_count, 3 * width)
    padded = extended(projected, (("row", 0), ("col", 1)), 1)
    mixed = depthwise(padded, conv_kernel, conv_bias, row_count, col_count)
    query = mixed[:, :, :width].astype(jnp.float32)
    key = mixed[:, :, width : 2 * width].astype(jnp.float32)
    value = mixed[:, :, 2 * width :].astype(jnp.float32)
    product = (key * value).astype(jnp.bfloat16)
    filt_pad = jnp.concatenate([jnp.zeros_like(long_filter), long_filter], axis=0)
    zero_band = jnp.zeros_like(filt_pad)
    filt_rev = jnp.concatenate([zero_band, jnp.flip(filt_pad, 0), zero_band], axis=0)
    my_start = lax.axis_index("row") * row_count
    empty_long = jnp.zeros((row_count, col_count, width), jnp.float32)
    total = empty_long
    piece = lax.all_gather(product, "row", axis=0, tiled=True)
    start = jnp.int32(0)
    piece_len = piece.shape[0]
    step_len = min(row_count, piece_len)
    for offset_row in range(0, piece_len, step_len):
        sub_piece = piece[offset_row : offset_row + step_len]
        sub_start = start + offset_row

        def work(running):
            toeplitz_block = toeplitz(filt_rev, my_start - sub_start, row_count, step_len)
            return running + jnp.einsum(
                "abc,bwc->awc", toeplitz_block, sub_piece, preferred_element_type=jnp.float32
            )

        def keep(running):
            return running

        total = lax.cond(sub_start < my_start + row_count, work, keep, total)
    gated = (query * (total + skip_gain * product.astype(jnp.float32))).astype(jnp.bfloat16)
    gated_flat = gated.reshape(row_count * col_count, width)
    final = jnp.dot(gated_flat, w_out, preferred_element_type=jnp.float32)
    return final.astype(jnp.bfloat16).reshape(row_count, col_count, width)


def solution(mesh):
    in_specs = (P("row", "col", None), P(), P(), P(), P(), P(), P())
    out_specs = P("row", "col", None)
    return jax.shard_map(
        on_device, mesh=mesh, in_specs=in_specs, out_specs=out_specs, check_vma=False
    )
```

profile of v0, /device:TPU:1, one launch (start us, length us, event | category | flops | bytes accessed | tf_op | source)
XLA Modules:
  0.0 115.1 jit_solution(9710104501801222011)
XLA Ops:
  6.5 0.0 copy-start
  6.5 0.0 all-gather.2.cloned.1.call-start
  6.5 1.0 copy-done
  7.6 1.6 %convolution_convert_fusion = bf16[1024,768]{1,0:T(8,128)(2,1)S(1)} fusion(bf16[1024,256]{1,0:T(8,128)(2,1)S(1)} %bitcast.18, bf16[256,768]{1,0:T(8,128)(2,1)} %param.12), kind=kOutput, calls=%fused_computation.9 | convolution fusion | flops 403439616 | bytes 2490368 | tf_op jit(solution)/shard_map/dot_general | solution.py:47
  9.2 1.3 %collective-permute-start = (bf16[1,32,768]{2,1,0:T(8,128)(2,1)S(1)}, bf16[1,32,768]{2,1,0:T(8,128)(2,1)S(1)}, u32[]{:S(2)}, u32[]{:S(2)}) collective-permute-start(bf16[1,32,768]{2,1,0:T(8,128)(2,1)S(1)} %get-tuple-element.63), channel_id=1, source_target_pairs={{0,128},{1,129},{2,130},{3,131},{4,132},{5,133},{6,134},{7,135},{8... | collective-permute-start | bytes 147464 | tf_op jit(solution)/shard_map/ppermute | solution.py:12
  10.5 5.1 %collective-permute-start.1 = (bf16[1,32,768]{2,1,0:T(8,128)(2,1)S(1)}, bf16[1,32,768]{2,1,0:T(8,128)(2,1)S(1)}, u32[]{:S(2)}, u32[]{:S(2)}) collective-permute-start(bf16[1,32,768]{2,1,0:T(8,128)(2,1)S(1)} %get-tuple-element.64), channel_id=1, source_target_pairs={{128,0},{129,1},{130,2},{131,3},{132,4},{133,5},{134,6},{135,7},{1... | collective-permute-start | bytes 147464 | tf_op jit(solution)/shard_map/ppermute | solution.py:15
  15.6 0.0 collective-permute-done
  15.6 0.9 collective-permute-done.1
  16.5 0.2 pad_maximum_fusion.6
  16.6 0.0 copy-start.6
  16.7 1.8 %collective-permute-start.2 = (bf16[34,1,768]{2,1,0:T(2,128)(2,1)S(1)}, bf16[34,1,768]{2,1,0:T(2,128)(2,1)S(1)}, u32[]{:S(2)}, u32[]{:S(2)}) collective-permute-start(bf16[34,1,768]{2,1,0:T(2,128)(2,1)S(1)} %get-tuple-element.61), channel_id=1, source_target_pairs={{0,1},{1,2},{2,3},{3,4},{4,5},{5,6},{6,7},{7,8},{8,9},{9,10},{10,1... | collective-permute-start | bytes 156680 | tf_op jit(solution)/shard_map/ppermute | solution.py:12
  18.5 1.3 %collective-permute-start.3 = (bf16[34,1,768]{2,1,0:T(2,128)(2,1)S(1)}, bf16[34,1,768]{2,1,0:T(2,128)(2,1)S(1)}, u32[]{:S(2)}, u32[]{:S(2)}) collective-permute-start(bf16[34,1,768]{2,1,0:T(2,128)(2,1)S(1)} %get-tuple-element.62), channel_id=1, source_target_pairs={{1,0},{2,1},{3,2},{4,3},{5,4},{6,5},{7,6},{8,7},{9,8},{10,9},{11,1... | collective-permute-start | bytes 156680 | tf_op jit(solution)/shard_map/ppermute | solution.py:15
  19.8 0.0 copy-done.4
  19.8 0.1 convert_reduce_fusion.8
  19.9 0.5 collective-permute-done.2
  20.4 3.8 %collective-permute-done.3 = bf16[34,1,768]{2,1,0:T(2,128)(2,1)S(1)} collective-permute-done((bf16[34,1,768]{2,1,0:T(2,128)(2,1)S(1)}, bf16[34,1,768]{2,1,0:T(2,128)(2,1)S(1)}, u32[]{:S(2)}, u32[]{:S(2)}) %collective-permute-start.3) | collective-permute-done | bytes 52256 | tf_op jit(solution)/shard_map/ppermute | solution.py:15
  24.2 1.2 %maximum_maximum_fusion = (bf16[34,33,768]{2,1,0:T(8,128)(2,1)S(1)}, bf16[34,33,768]{2,1,0:T(8,128)(2,1)S(1)}) fusion(bf16[1,32,768]{2,1,0:T(8,128)(2,1)S(1)} %collective-permute-done.1, bf16[32,32,768]{2,1,0:T(8,128)(2,1)S(1)} %bitcast.20, bf16[1,32,768]{2,1,0:T(8,128)(2,1)S(1)} %collective-permute-done, bf16[34,1,768]{2,1,0:T(2,128)(2,1)S(1)} %collective-permute-done.2, ...), kind=kLoop, calls=%fused_computation.7 | loop fusion | flops 13787136 | bytes 5222400 | tf_op jit(solution)/shard_map/concatenate | solution.py:16
  25.5 0.0 copy-done.6
  25.5 0.0 copy-start.5
  25.5 4.1 %add_convert_fusion = bf16[32,32,768]{2,1,0:T(8,128)(2,1)S(1)} fusion(bf16[32,32,768]{2,1,0:T(8,128)(2,1)S(1)} %bitcast.21, bf16[34,33,768]{2,1,0:T(8,128)(2,1)S(1)} %get-tuple-element.60, bf16[1,32,768]{2,1,0:T(8,128)(2,1)S(1)} %collective-permute-done.1, bf16[34,33,768]{2,1,0:T(8,128)(2,1)S(1)} %get-tuple-element.59, ...), kind=kLoop, calls=%fused_computation.6 | loop fusion | flops 23592960 | bytes 12711936 | tf_op jit(solution)/shard_map/convert_element_type | solution.py:28
  29.6 0.9 multiply_convert_fusion.1
  30.5 0.0 all-gather.2.cloned.1.call-update
  30.6 0.0 copy-done.5
  30.6 0.1 rev.4
  30.7 22.5 %all-gather.2.cloned.1.call-done = bf16[64,32,256]{2,1,0:T(8,128)(2,1)} async-done(((bf16[32,32,256]{2,1,0:T(8,128)(2,1)}), bf16[64,32,256]{2,1,0:T(8,128)(2,1)}) %all-gather.2.cloned.1.call-update) | async-done | bytes 1048592 | tf_op jit(solution)/shard_map/all_gather | solution.py:61
  53.2 24.2 %conditional.2 = (f32[32,32,256]{1,0,2:T(8,128)}) conditional(s32[]{:T(128)} %convert_element_type.91, () %tuple.17, (s32[]{:T(128)}, bf16[384,256]{1,0:T(8,128)(2,1)S(1)}, bf16[64,32,256]{2,1,0:T(8,128)(2,1)}) %tuple.18), branch_computations={%region_0.1_spmd, %region_1.2_spmd} | conditional | flops 16777220 | bytes 20984918 | solution.py:78
  53.3 0.1 tile.4
  53.4 1.3 %tile.10 = bf16[2079,256]{1,0:T(8,128)(2,1)} reshape(bf16[33,63,256]{2,1,0:T(8,128)(2,1)S(1)} %tile.4) | data formatting | bytes 2128896 | tf_op jit(solution)/shard_map/cond/branch_1_fun/tile | solution.py:39
  54.7 2.5 %slice.133 = bf16[1984,256]{1,0:T(8,128)(2,1)} slice(bf16[2079,256]{1,0:T(8,128)(2,1)} %tile.10), slice={[31:2015], [0:256]} | slice | bytes 2031616 | tf_op jit(solution)/shard_map/cond/branch_1_fun/slice | solution.py:40
  57.2 2.3 %reshape.24 = bf16[32,62,256]{2,1,0:T(8,128)(2,1)} reshape(bf16[1984,256]{1,0:T(8,128)(2,1)} %slice.133) | data formatting | bytes 2031616 | tf_op jit(solution)/shard_map/cond/branch_1_fun/reshape | solution.py:41
  59.5 1.9 %slice.134 = bf16[32,32,256]{2,1,0:T(8,128)(2,1)} slice(bf16[32,62,256]{2,1,0:T(8,128)(2,1)} %reshape.24), slice={[0:32], [0:32], [0:256]} | slice | bytes 1048576 | tf_op jit(solution)/shard_map/cond/branch_1_fun/slice | solution.py:41
  61.4 4.6 %copy.29 = bf16[32,32,256]{1,0,2:T(8,128)(2,1)} copy(bf16[32,32,256]{2,1,0:T(8,128)(2,1)} %slice.134) | data formatting | bytes 1048576 | tf_op jit(solution)/shard_map/cond
  66.0 0.0 copy-done.1
  66.0 6.5 %copy.24 = bf16[64,32,256]{1,0,2:T(8,128)(2,1)} copy(bf16[64,32,256]{2,1,0:T(8,128)(2,1)S(1)} %copy-done.1) | data formatting | bytes 2097152 | tf_op jit(solution)/shard_map
  72.5 4.9 %convolution_bitcast_fusion = f32[32,32,256]{1,0,2:T(8,128)} fusion(bf16[32,32,256]{1,0,2:T(8,128)(2,1)} %copy.29, bf16[64,32,256]{1,0,2:T(8,128)(2,1)} %copy.24), kind=kOutput, calls=%fused_computation | convolution fusion | flops 16777216 | bytes 5242880 | tf_op jit(solution)/shard_map/cond/branch_1_fun/abc,bwc->awc/dot_general | solution.py:71
  77.4 28.8 %conditional.3 = (f32[32,32,256]{2,1,0:T(8,128)S(1)}) conditional(s32[]{:T(128)} %convert_element_type.90, f32[32,32,256]{1,0,2:T(8,128)} %get-tuple-element.67, (s32[]{:T(128)}, bf16[384,256]{1,0:T(8,128)(2,1)S(1)}, bf16[64,32,256]{2,1,0:T(8,128)(2,1)}, f32[32,32,256]{1,0,2:T(8,128)}) %tuple.19), branch_computations={%region_2.3_spmd, %region_3.4_spmd} | conditional | flops 17039364 | bytes 27276386 | solution.py:78
  77.4 0.1 tile.11
  77.6 1.3 %tile.12 = bf16[2079,256]{1,0:T(8,128)(2,1)} reshape(bf16[33,63,256]{2,1,0:T(8,128)(2,1)S(1)} %tile.11) | data formatting | bytes 2128896 | tf_op jit(solution)/shard_map/cond/branch_1_fun/tile | solution.py:39
  78.9 2.4 %slice.136 = bf16[1984,256]{1,0:T(8,128)(2,1)} slice(bf16[2079,256]{1,0:T(8,128)(2,1)} %tile.12), slice={[31:2015], [0:256]} | slice | bytes 2031616 | tf_op jit(solution)/shard_map/cond/branch_1_fun/slice | solution.py:40
  81.3 2.4 %reshape.25 = bf16[32,62,256]{2,1,0:T(8,128)(2,1)} reshape(bf16[1984,256]{1,0:T(8,128)(2,1)} %slice.136) | data formatting | bytes 2031616 | tf_op jit(solution)/shard_map/cond/branch_1_fun/reshape | solution.py:41
  83.7 1.9 %slice.137 = bf16[32,32,256]{2,1,0:T(8,128)(2,1)} slice(bf16[32,62,256]{2,1,0:T(8,128)(2,1)} %reshape.25), slice={[0:32], [0:32], [0:256]} | slice | bytes 1048576 | tf_op jit(solution)/shard_map/cond/branch_1_fun/slice | solution.py:41
  85.5 4.6 %copy.30 = bf16[32,32,256]{1,0,2:T(8,128)(2,1)} copy(bf16[32,32,256]{2,1,0:T(8,128)(2,1)} %slice.137) | data formatting | bytes 1048576 | tf_op jit(solution)/shard_map/cond
  90.1 6.5 %copy.25 = bf16[64,32,256]{1,0,2:T(8,128)(2,1)} copy(bf16[64,32,256]{2,1,0:T(8,128)(2,1)S(1)} %copy-done.2) | data formatting | bytes 2097152 | tf_op jit(solution)/shard_map
  96.6 6.1 %bitcast_add_fusion = f32[32,32,256]{1,0,2:T(8,128)} fusion(f32[32,32,256]{1,0,2:T(8,128)} %get-tuple-element.30, bf16[32,32,256]{1,0,2:T(8,128)(2,1)} %copy.30, bf16[64,32,256]{1,0,2:T(8,128)(2,1)} %copy.25), kind=kOutput, calls=%fused_computation.3 | convolution fusion | flops 17039360 | bytes 9437184 | tf_op jit(solution)/shard_map/cond/branch_1_fun/abc,bwc->awc/dot_general | solution.py:71
  102.7 3.5 %copy.28 = f32[32,32,256]{2,1,0:T(8,128)S(1)} copy(f32[32,32,256]{1,0,2:T(8,128)} %bitcast_add_fusion) | data formatting | bytes 2097152 | tf_op jit(solution)/shard_map/cond | solution.py:78
  106.3 0.3 multiply_convert_fusion
  106.5 0.6 copy-done.3
  107.1 1.1 convolution_convert_fusion.1
  (13 shorter events, 0.1 us)
Async XLA Ops:
  6.5 1.0 copy-start
  6.5 13.3 %copy-start.4 = (bf16[3,3,768]{2,1,0:T(4,128)(2,1)S(1)}, bf16[3,3,768]{2,1,0:T(4,128)(2,1)}, u32[]{:S(2)}) copy-start(bf16[3,3,768]{2,1,0:T(4,128)(2,1)} %param.13) | copy-start | bytes 41476
  6.5 46.7 %all-gather.2.cloned.1.call-start = ((), (), s32[]{:S(2)}) async-start(), calls=%async_computation | async-start | bytes 1572864 | tf_op jit(solution)/shard_map/all_gather | solution.py:61
  9.2 6.5 %collective-permute-start = (bf16[1,32,768]{2,1,0:T(8,128)(2,1)S(1)}, bf16[1,32,768]{2,1,0:T(8,128)(2,1)S(1)}, u32[]{:S(2)}, u32[]{:S(2)}) collective-permute-start(bf16[1,32,768]{2,1,0:T(8,128)(2,1)S(1)} %get-tuple-element.63), channel_id=1, source_target_pairs={{0,128},{1,129},{2,130},{3,131},{4,132},{5,133},{6,134},{7,135},{8... | collective-permute-start | bytes 147464 | tf_op jit(solution)/shard_map/ppermute | solution.py:12
  10.5 6.0 %collective-permute-start.1 = (bf16[1,32,768]{2,1,0:T(8,128)(2,1)S(1)}, bf16[1,32,768]{2,1,0:T(8,128)(2,1)S(1)}, u32[]{:S(2)}, u32[]{:S(2)}) collective-permute-start(bf16[1,32,768]{2,1,0:T(8,128)(2,1)S(1)} %get-tuple-element.64), channel_id=1, source_target_pairs={{128,0},{129,1},{130,2},{131,3},{132,4},{133,5},{134,6},{135,7},{1... | collective-permute-start | bytes 147464 | tf_op jit(solution)/shard_map/ppermute | solution.py:15
  16.6 8.8 %copy-start.6 = (f32[768]{0:T(1024)S(1)}, f32[768]{0:T(1024)}, u32[]{:S(2)}) copy-start(f32[768]{0:T(1024)} %param.14) | copy-start | bytes 9220
  16.7 3.8 %collective-permute-start.2 = (bf16[34,1,768]{2,1,0:T(2,128)(2,1)S(1)}, bf16[34,1,768]{2,1,0:T(2,128)(2,1)S(1)}, u32[]{:S(2)}, u32[]{:S(2)}) collective-permute-start(bf16[34,1,768]{2,1,0:T(2,128)(2,1)S(1)} %get-tuple-element.61), channel_id=1, source_target_pairs={{0,1},{1,2},{2,3},{3,4},{4,5},{5,6},{6,7},{7,8},{8,9},{9,10},{10,1... | collective-permute-start | bytes 156680 | tf_op jit(solution)/shard_map/ppermute | solution.py:12
  18.5 5.7 %collective-permute-start.3 = (bf16[34,1,768]{2,1,0:T(2,128)(2,1)S(1)}, bf16[34,1,768]{2,1,0:T(2,128)(2,1)S(1)}, u32[]{:S(2)}, u32[]{:S(2)}) collective-permute-start(bf16[34,1,768]{2,1,0:T(2,128)(2,1)S(1)} %get-tuple-element.62), channel_id=1, source_target_pairs={{1,0},{2,1},{3,2},{4,3},{5,4},{6,5},{7,6},{8,7},{9,8},{10,9},{11,1... | collective-permute-start | bytes 156680 | tf_op jit(solution)/shard_map/ppermute | solution.py:15
  25.5 5.1 %copy-start.5 = (bf16[64,256]{1,0:T(8,128)(2,1)S(1)}, bf16[64,256]{1,0:T(8,128)(2,1)}, u32[]{:S(2)}) copy-start(bf16[64,256]{1,0:T(8,128)(2,1)} %param.15) | copy-start | bytes 98308
  57.2 8.8 %copy-start.1 = (bf16[64,32,256]{2,1,0:T(8,128)(2,1)S(1)}, bf16[64,32,256]{2,1,0:T(8,128)(2,1)}, u32[]{:S(2)}) copy-start(bf16[64,32,256]{2,1,0:T(8,128)(2,1)} %get-tuple-element.44) | copy-start | bytes 3145732 | tf_op jit(solution)/shard_map/cond
  77.4 28.8 %copy-start.7 = (f32[256]{0:T(256)S(1)}, f32[256]{0:T(256)}, u32[]{:S(2)}) copy-start(f32[256]{0:T(256)} %param.16) | copy-start | bytes 3076
  81.3 8.8 %copy-start.2 = (bf16[64,32,256]{2,1,0:T(8,128)(2,1)S(1)}, bf16[64,32,256]{2,1,0:T(8,128)(2,1)}, u32[]{:S(2)}) copy-start(bf16[64,32,256]{2,1,0:T(8,128)(2,1)} %get-tuple-element.47) | copy-start | bytes 3145732 | tf_op jit(solution)/shard_map/cond
  106.2 0.9 copy-start.3
Sparse Core Ops, SparseCore 0:
  30.7 22.5 all-gather.1
where the time goes:
time: 116 us; the launch traced here: 115 us
  local copies, waits for them, and re-layouts  43.7 us (38%)
  waiting for transfers between devices  27.7 us (24%)
  matrix products  13.7 us (12%)
  between operations  13.6 us (12%)
  starting transfers between devices  9.57 us (8%)
  other arithmetic  6.79 us (6%)
    all_gather x1, waiting for transfers between devices, on_device(): piece = lax.all_gather(product, 'row', axis=0, tiled=True)  22.5 us
    another operation x2, local copies, waits for them, and re-layouts  13 us
    dot_general x2, matrix products, work(): jnp.einsum('abc,bwc->awc', toeplitz_block, sub_piece, preferred_element_t...  11.1 us
    cond x6, local copies, waits for them, and re-layouts  9.15 us
    ppermute x2, starting transfers between devices, extended(): lax.ppermute(lax.slice_in_dim(block, 0, width, axis=dim), axis, backward)  6.44 us
    slice x2, local copies, waits for them, and re-layouts, toeplitz(): strided = tiled[out_count - 1:out_count - 1 + out_count * (length - 1)]  4.91 us
    reshape x2, local copies, waits for them, and re-layouts, toeplitz(): strided.reshape(out_count, length - 1, filt_rev.shape[1])[:, :src_count]  4.73 us
    ppermute x2, waiting for transfers between devices, extended(): lax.ppermute(lax.slice_in_dim(block, 0, width, axis=dim), axis, backward)  4.65 us
  transfers between devices with their start and end apart: 5, of which 4 were waited for; matrix products, arithmetic and copies ran while one was open for 0% of the time, Pallas kernels for 0%

commit v1 on v0

v1 whole, which is shorter than its diff:
```python
import functools

import jax
import jax.numpy as jnp
from jax import lax
from jax.experimental import pallas as pl
from jax.experimental.pallas import tpu as pltpu
from jax.sharding import PartitionSpec as P


def extended(block, sides, width):
    for axis, dim in sides:
        count = lax.axis_size(axis)
        forward = [(i, i + 1) for i in range(count - 1)]
        backward = [(target, source) for source, target in forward]
        low = lax.ppermute(
            lax.slice_in_dim(block, block.shape[dim] - width, None, axis=dim), axis, forward
        )
        high = lax.ppermute(lax.slice_in_dim(block, 0, width, axis=dim), axis, backward)
        block = jnp.concatenate([low, block, high], axis=dim)
    return block


def depthwise(padded, kernel, bias, height, span):
    total = jnp.zeros((height, span, padded.shape[2]), jnp.float32) + bias
    for row_off in range(3):
        for col_off in range(3):
            window = padded[row_off : row_off + height, col_off : col_off + span, :].astype(
                jnp.float32
            )
            total = total + window * kernel[row_off, col_off].astype(jnp.float32)
    return total.astype(jnp.bfloat16)


def longconv_kernel(rows, span, prev_ref, own_ref, q_ref, filt_ref, gain_ref, wout_ref, out_ref,
                    ext_ref, fb_ref, qf_ref, gated_ref):
    count = rows * span
    width = own_ref.shape[1]
    ext_ref[0:count, :] = prev_ref[...].astype(jnp.float32)
    ext_ref[count : 2 * count, :] = own_ref[...].astype(jnp.float32)
    qf_ref[...] = q_ref[...].astype(jnp.float32)
    for lag in range(2 * rows):
        fb_ref[lag] = jnp.broadcast_to(filt_ref[lag : lag + 1, :].astype(jnp.float32), (8, width))
    lane_groups = width // 128

    def chunk(i, carry):
        lanes = pl.ds(pl.multiple_of((i % lane_groups) * 128, 128), 128)
        w0 = pl.multiple_of((i // lane_groups) * 8, 8)
        acc = [None] * rows
        for src in range(2 * rows):
            x = ext_ref[pl.ds(src * span + w0, 8), lanes]
            for a in range(max(0, src - rows), rows):
                term = fb_ref[rows + a - src, :, lanes] * x
                acc[a] = term if acc[a] is None else acc[a] + term
        gain = jnp.broadcast_to(gain_ref[:, lanes], (8, 128))
        for a in range(rows):
            own = ext_ref[pl.ds(count + a * span + w0, 8), lanes]
            q = qf_ref[pl.ds(a * span + w0, 8), lanes]
            gated_ref[pl.ds(a * span + w0, 8), lanes] = q * (acc[a] + gain * own)
        return carry

    lax.fori_loop(0, (span // 8) * lane_groups, chunk, 0)
    out_ref[...] = jnp.dot(
        gated_ref[...].astype(jnp.bfloat16), wout_ref[...], preferred_element_type=jnp.float32
    ).astype(out_ref.dtype)


def on_device(image_tokens, w_in, conv_kernel, conv_bias, long_filter, skip_gain, w_out):
    row_count, col_count, width = image_tokens.shape
    tokens = extended(image_tokens, (("row", 0), ("col", 1)), 1)
    projected = jnp.dot(
        tokens.reshape(-1, width), w_in, preferred_element_type=jnp.float32
    ).astype(jnp.bfloat16)
    projected = projected.reshape(row_count + 2, col_count + 2, 3 * width)
    mixed = depthwise(projected, conv_kernel, conv_bias, row_count, col_count)
    query = mixed[:, :, :width]
    key = mixed[:, :, width : 2 * width].astype(jnp.float32)
    value = mixed[:, :, 2 * width :].astype(jnp.float32)
    product = (key * value).astype(jnp.bfloat16)
    count = lax.axis_size("row")
    prev = lax.ppermute(product, "row", [(i, i + 1) for i in range(count - 1)])
    flat = row_count * col_count
    vmem = pl.BlockSpec(memory_space=pltpu.VMEM)
    out = pl.pallas_call(
        functools.partial(longconv_kernel, row_count, col_count),
        out_shape=jax.ShapeDtypeStruct((flat, width), jnp.bfloat16),
        in_specs=[vmem] * 6,
        out_specs=vmem,
        scratch_shapes=[
            pltpu.VMEM((2 * flat, width), jnp.float32),
            pltpu.VMEM((2 * row_count, 8, width), jnp.float32),
            pltpu.VMEM((flat, width), jnp.float32),
            pltpu.VMEM((flat, width), jnp.float32),
        ],
    )(
        prev.reshape(flat, width),
        product.reshape(flat, width),
        query.reshape(flat, width),
        long_filter,
        skip_gain.reshape(1, width),
        w_out,
    )
    return out.reshape(row_count, col_count, width)


def solution(mesh):
    in_specs = (P("row", "col", None), P(), P(), P(), P(), P(), P())
    out_specs = P("row", "col", None)
    return jax.shard_map(
        on_device, mesh=mesh, in_specs=in_specs, out_specs=out_specs, check_vma=False
    )
```

time: 116 us -> 42.2 us (0.36)
  the two profiles are of different devices: /device:TPU:1 before, /device:TPU:127 now
where the time goes in v1:
time: 42.2 us; the launch traced here: 41.9 us
  starting transfers between devices  11.8 us (28%)
  waiting for transfers between devices  9.24 us (22%)
  Pallas kernels  7.19 us (17%)
  local copies, waits for them, and re-layouts  6.22 us (15%)
  other arithmetic  5.34 us (13%)
  matrix products  1.87 us (4%)
    ppermute x2, waiting for transfers between devices, extended(): lax.ppermute(lax.slice_in_dim(block, 0, width, axis=dim), axis, backward)  7.24 us
    pallas_call x1, Pallas kernels, on_device(): pl.pallas_call(functools.partial(longconv_kernel, row_count, col_count),...  7.19 us
    ppermute x2, starting transfers between devices, extended(): lax.ppermute(lax.slice_in_dim(block, block.shape[dim] - width, None, axis...  5.61 us
    ppermute x2, starting transfers between devices, extended(): lax.ppermute(lax.slice_in_dim(block, 0, width, axis=dim), axis, backward)  4.95 us
    convert_element_type x1, other arithmetic, depthwise(): return total.astype(jnp.bfloat16)  3.85 us
    reshape x1, local copies, waits for them, and re-layouts, on_device(): projected = projected.reshape(row_count + 2, col_count + 2, 3 * width)  2.47 us
    ppermute x1, waiting for transfers between devices, on_device(): prev = lax.ppermute(product, 'row', [(i, i + 1) for i in range(count - 1)])  1.99 us
    unnamed x10, local copies, waits for them, and re-layouts  1.88 us
  transfers between devices with their start and end apart: 5, of which 2 were waited for; matrix products, arithmetic and copies ran while one was open for 7% of the time, Pallas kernels for 0%

profile of v1, /device:TPU:127, one launch (start us, length us, event | category | flops | bytes accessed | tf_op | source)
XLA Modules:
  0.0 41.9 jit_solution(11214577747567830106)
XLA Ops:
  0.0 0.0 copy-start
  0.0 0.8 %fusion.1 = (bf16[1,32,256]{2,1,0:T(8,128)(2,1)S(1)}, bf16[1,32,256]{2,1,0:T(8,128)(2,1)S(1)}) fusion(bf16[32,32,256]{2,1,0:T(8,128)(2,1)} %param.7), kind=kLoop, calls=%fused_computation.17 | loop fusion | bytes 65536 | tf_op jit(solution)/shard_map/slice | solution.py:19
  0.8 1.3 %collective-permute-start = (bf16[1,32,256]{2,1,0:T(8,128)(2,1)S(1)}, bf16[1,32,256]{2,1,0:T(8,128)(2,1)S(1)}, u32[]{:S(2)}, u32[]{:S(2)}) collective-permute-start(bf16[1,32,256]{2,1,0:T(8,128)(2,1)S(1)} %get-tuple-element.17), channel_id=1, source_target_pairs={{0,128},{1,129},{2,130},{3,131},{4,132},{5,133},{6,134},{7,135},{8... | collective-permute-start | bytes 49160 | tf_op jit(solution)/shard_map/ppermute | solution.py:16
  2.1 3.0 %collective-permute-start.1 = (bf16[1,32,256]{2,1,0:T(8,128)(2,1)S(1)}, bf16[1,32,256]{2,1,0:T(8,128)(2,1)S(1)}, u32[]{:S(2)}, u32[]{:S(2)}) collective-permute-start(bf16[1,32,256]{2,1,0:T(8,128)(2,1)S(1)} %get-tuple-element.16), channel_id=1, source_target_pairs={{128,0},{129,1},{130,2},{131,3},{132,4},{133,5},{134,6},{135,7},{1... | collective-permute-start | bytes 49160 | tf_op jit(solution)/shard_map/ppermute | solution.py:19
  5.1 0.0 collective-permute-done
  5.1 1.1 %constant_dynamic-update-slice_fusion.1 = bf16[34,32,256]{2,1,0:T(8,128)(2,1)S(1)} fusion(bf16[34,32,256]{2,1,0:T(8,128)(2,1)S(1)} %constant_dynamic-update-slice_fusion.2, bf16[32,32,256]{2,1,0:T(8,128)(2,1)} %param.7), kind=kLoop, calls=%fused_computation.5 | loop fusion | bytes 1048576
  6.2 0.0 collective-permute-done.1
  6.2 0.1 fusion
  6.3 4.3 %collective-permute-start.2 = (bf16[34,1,256]{2,1,0:T(2,128)(2,1)S(1)}, bf16[34,1,256]{2,1,0:T(2,128)(2,1)S(1)}, u32[]{:S(2)}, u32[]{:S(2)}) collective-permute-start(bf16[34,1,256]{2,1,0:T(2,128)(2,1)S(1)} %get-tuple-element.14), channel_id=1, source_target_pairs={{0,1},{1,2},{2,3},{3,4},{4,5},{5,6},{6,7},{7,8},{8,9},{9,10},{10,1... | collective-permute-start | bytes 52232 | tf_op jit(solution)/shard_map/ppermute | solution.py:16
  10.6 1.9 %collective-permute-start.3 = (bf16[34,1,256]{2,1,0:T(2,128)(2,1)S(1)}, bf16[34,1,256]{2,1,0:T(2,128)(2,1)S(1)}, u32[]{:S(2)}, u32[]{:S(2)}) collective-permute-start(bf16[34,1,256]{2,1,0:T(2,128)(2,1)S(1)} %get-tuple-element.15), channel_id=1, source_target_pairs={{1,0},{2,1},{3,2},{4,3},{5,4},{6,5},{7,6},{8,7},{9,8},{10,9},{11,1... | collective-permute-start | bytes 52232 | tf_op jit(solution)/shard_map/ppermute | solution.py:19
  12.6 0.9 %convert_reduce_fusion.8 = (f32[768]{0:T(1024)S(1)}, f32[768]{0:T(1024)S(1)}, f32[768]{0:T(1024)S(1)}, f32[768]{0:T(1024)S(1)}, f32[768]{0:T(1024)S(1)}, /*index...) fusion(bf16[3,3,768]{2,1,0:T(4,128)(2,1)} %param.9), kind=kLoop, calls=%fused_computation.15 | loop fusion | flops 6912 | bytes 41472 | tf_op jit(solution)/shard_map/mul | solution.py:31
  13.5 0.0 collective-permute-done.2
  13.5 7.2 %collective-permute-done.3 = bf16[34,1,256]{2,1,0:T(2,128)(2,1)S(1)} collective-permute-done((bf16[34,1,256]{2,1,0:T(2,128)(2,1)S(1)}, bf16[34,1,256]{2,1,0:T(2,128)(2,1)S(1)}, u32[]{:S(2)}, u32[]{:S(2)}) %collective-permute-start.3) | collective-permute-done | bytes 17440 | tf_op jit(solution)/shard_map/ppermute | solution.py:19
  20.8 0.4 pad_maximum_fusion
  21.2 0.2 reshape.22
  21.3 0.0 copy-done
  21.3 1.9 %convolution_convert_fusion = bf16[1156,768]{1,0:T(8,128)(2,1)} fusion(bf16[1156,256]{1,0:T(8,128)(2,1)S(1)} %reshape.22, bf16[256,768]{1,0:T(8,128)(2,1)S(1)} %copy-done), kind=kOutput, calls=%fused_computation | convolution fusion | flops 455445504 | bytes 2760704 | tf_op jit(solution)/shard_map/dot_general | solution.py:71
  23.2 0.0 copy-start.3
  23.2 2.5 %reshape.23 = bf16[34,34,768]{2,1,0:T(8,128)(2,1)S(1)} reshape(bf16[1156,768]{1,0:T(8,128)(2,1)} %convolution_convert_fusion) | data formatting | bytes 3551232 | tf_op jit(solution)/shard_map/reshape | solution.py:74
  25.7 0.0 copy-done.3
  25.7 3.9 %add_convert_fusion = bf16[32,32,768]{2,1,0:T(8,128)(2,1)S(1)} fusion(bf16[34,34,768]{2,1,0:T(8,128)(2,1)S(1)} %reshape.23, f32[768]{0:T(1024)S(1)} %get-tuple-element.12, f32[768]{0:T(1024)S(1)} %get-tuple-element.13, f32[768]{0:T(1024)S(1)} %get-tuple-element.6, f32[768]{0:T(1024)S(1)} %get-tuple-element.7, f32[768]{0:T(1024)S(1)} %get-tuple-element.8, ...), kind=kLoop, calls=%fused_computation.1 | loop fusion | flops 22020096 | bytes 15759360 | tf_op jit(solution)/shard_map/convert_element_type | solution.py:32
  29.6 0.2 multiply_convert_fusion
  29.7 0.0 copy-start.1
  29.7 1.3 %collective-permute-start.4 = (bf16[32,32,256]{2,1,0:T(8,128)(2,1)S(1)}, bf16[32,32,256]{2,1,0:T(8,128)(2,1)S(1)}, u32[]{:S(2)}, u32[]{:S(2)}) collective-permute-start(bf16[32,32,256]{2,1,0:T(8,128)(2,1)S(1)} %multiply_convert_fusion), channel_id=1, source_target_pairs={{0,128},{1,129},{2,130},{3,131},{4,132},{5,133},{6,134},{7,135},{8... | collective-permute-start | bytes 1572872 | tf_op jit(solution)/shard_map/ppermute | solution.py:81
  31.0 0.9 %slice.113 = bf16[32,32,256]{2,1,0:T(8,128)(2,1)} slice(bf16[32,32,768]{2,1,0:T(8,128)(2,1)S(1)} %add_convert_fusion), slice={[0:32], [0:32], [0:256]} | slice | bytes 1048576 | tf_op jit(solution)/shard_map/slice | solution.py:76
  31.9 2.0 %collective-permute-done.4 = bf16[32,32,256]{2,1,0:T(8,128)(2,1)S(1)} collective-permute-done((bf16[32,32,256]{2,1,0:T(8,128)(2,1)S(1)}, bf16[32,32,256]{2,1,0:T(8,128)(2,1)S(1)}, u32[]{:S(2)}, u32[]{:S(2)}) %collective-permute-start.4) | collective-permute-done | bytes 524320 | tf_op jit(solution)/shard_map/ppermute | solution.py:81
  33.9 0.0 copy-start.2
  33.9 0.0 copy-done.1
  33.9 0.8 %copy-done.2 = bf16[32,32,256]{2,1,0:T(8,128)(2,1)} copy-done((bf16[32,32,256]{2,1,0:T(8,128)(2,1)}, bf16[32,32,256]{2,1,0:T(8,128)(2,1)S(1)}, u32[]{:S(2)}) %copy-start.2) | copy-done | bytes 524312
  34.7 7.2 %shard_map.73 = bf16[1024,256]{1,0:T(8,128)(2,1)} custom-call(bf16[1024,256]{1,0:T(8,128)(2,1)} %bitcast.9, bf16[1024,256]{1,0:T(8,128)(2,1)} %bitcast.7, bf16[1024,256]{1,0:T(8,128)(2,1)} %bitcast.8, bf16[64,256]{1,0:T(8,128)(2,1)} %filt_ref.1, f32[1,256]{1,0:T(1,128)} %bitcast.10, bf16[256,256]{1,0:T(8,128)(2,1)} %wout_ref.1), custom_call_target="tpu_custom_call" | custom-call | tf_op jit(solution)/shard_map/pallas_call | solution.py:84
  (2 shorter events, 0.0 us)
Async XLA Ops:
  0.0 21.3 %copy-start = (bf16[256,768]{1,0:T(8,128)(2,1)S(1)}, bf16[256,768]{1,0:T(8,128)(2,1)}, u32[]{:S(2)}) copy-start(bf16[256,768]{1,0:T(8,128)(2,1)} %param.8) | copy-start | bytes 1179652
  0.8 4.3 %collective-permute-start = (bf16[1,32,256]{2,1,0:T(8,128)(2,1)S(1)}, bf16[1,32,256]{2,1,0:T(8,128)(2,1)S(1)}, u32[]{:S(2)}, u32[]{:S(2)}) collective-permute-start(bf16[1,32,256]{2,1,0:T(8,128)(2,1)S(1)} %get-tuple-element.17), channel_id=1, source_target_pairs={{0,128},{1,129},{2,130},{3,131},{4,132},{5,133},{6,134},{7,135},{8... | collective-permute-start | bytes 49160 | tf_op jit(solution)/shard_map/ppermute | solution.py:16
  2.1 4.1 %collective-permute-start.1 = (bf16[1,32,256]{2,1,0:T(8,128)(2,1)S(1)}, bf16[1,32,256]{2,1,0:T(8,128)(2,1)S(1)}, u32[]{:S(2)}, u32[]{:S(2)}) collective-permute-start(bf16[1,32,256]{2,1,0:T(8,128)(2,1)S(1)} %get-tuple-element.16), channel_id=1, source_target_pairs={{128,0},{129,1},{130,2},{131,3},{132,4},{133,5},{134,6},{135,7},{1... | collective-permute-start | bytes 49160 | tf_op jit(solution)/shard_map/ppermute | solution.py:19
  6.3 7.2 %collective-permute-start.2 = (bf16[34,1,256]{2,1,0:T(2,128)(2,1)S(1)}, bf16[34,1,256]{2,1,0:T(2,128)(2,1)S(1)}, u32[]{:S(2)}, u32[]{:S(2)}) collective-permute-start(bf16[34,1,256]{2,1,0:T(2,128)(2,1)S(1)} %get-tuple-element.14), channel_id=1, source_target_pairs={{0,1},{1,2},{2,3},{3,4},{4,5},{5,6},{6,7},{7,8},{8,9},{9,10},{10,1... | collective-permute-start | bytes 52232 | tf_op jit(solution)/shard_map/ppermute | solution.py:16
  10.6 10.1 %collective-permute-start.3 = (bf16[34,1,256]{2,1,0:T(2,128)(2,1)S(1)}, bf16[34,1,256]{2,1,0:T(2,128)(2,1)S(1)}, u32[]{:S(2)}, u32[]{:S(2)}) collective-permute-start(bf16[34,1,256]{2,1,0:T(2,128)(2,1)S(1)} %get-tuple-element.15), channel_id=1, source_target_pairs={{1,0},{2,1},{3,2},{4,3},{5,4},{6,5},{7,6},{8,7},{9,8},{10,9},{11,1... | collective-permute-start | bytes 52232 | tf_op jit(solution)/shard_map/ppermute | solution.py:19
  23.2 2.5 %copy-start.3 = (f32[768]{0:T(1024)S(1)}, f32[768]{0:T(1024)}, u32[]{:S(2)}) copy-start(f32[768]{0:T(1024)} %param.10) | copy-start | bytes 9220
  29.7 4.2 %copy-start.1 = (bf16[32,32,256]{2,1,0:T(8,128)(2,1)}, bf16[32,32,256]{2,1,0:T(8,128)(2,1)S(1)}, u32[]{:S(2)}) copy-start(bf16[32,32,256]{2,1,0:T(8,128)(2,1)S(1)} %multiply_convert_fusion) | copy-start | bytes 1572868
  29.7 4.1 %collective-permute-start.4 = (bf16[32,32,256]{2,1,0:T(8,128)(2,1)S(1)}, bf16[32,32,256]{2,1,0:T(8,128)(2,1)S(1)}, u32[]{:S(2)}, u32[]{:S(2)}) collective-permute-start(bf16[32,32,256]{2,1,0:T(8,128)(2,1)S(1)} %multiply_convert_fusion), channel_id=1, source_target_pairs={{0,128},{1,129},{2,130},{3,131},{4,132},{5,133},{6,134},{7,135},{8... | collective-permute-start | bytes 1572872 | tf_op jit(solution)/shard_map/ppermute | solution.py:81
  33.9 0.8 %copy-start.2 = (bf16[32,32,256]{2,1,0:T(8,128)(2,1)}, bf16[32,32,256]{2,1,0:T(8,128)(2,1)S(1)}, u32[]{:S(2)}) copy-start(bf16[32,32,256]{2,1,0:T(8,128)(2,1)S(1)} %collective-permute-done.4) | copy-start | bytes 1572868

commit v2 on v1

--- a/solution.py
+++ b/solution.py
@@ -65,22 +65,134 @@
     ).astype(out_ref.dtype)
 
 
+def front_kernel(rows, span, pitch, send_ref, x_ref, w_ref, k_ref, b_ref, q_out, p_out,
+                 halo, pext, kb, bb, hp, send_sem, recv_sem):
+    width = x_ref.shape[2]
+    wide = w_ref.shape[1]
+    r = lax.axis_index("row")
+    c = lax.axis_index("col")
+    ncol = lax.axis_size("col")
+    partner = 1 - r
+    mesh_id = pl.DeviceIdType.MESH
+
+    halo[...] = jnp.zeros_like(halo)
+    barrier = pltpu.get_barrier_semaphore()
+    right = lax.rem(c + 1, ncol)
+    left = lax.rem(c + ncol - 1, ncol)
+    peers = ((partner, c), (r, right), (r, left), (partner, right), (partner, left))
+    for dev in peers:
+        pl.semaphore_signal(barrier, 1, device_id=dev, device_id_type=mesh_id)
+    pl.semaphore_wait(barrier, len(peers))
+
+    out = [
+        pltpu.make_async_remote_copy(send_ref.at[slot], halo.at[slot], send_sem.at[slot],
+                                     recv_sem.at[slot], device_id=dev, device_id_type=mesh_id)
+        for slot, dev in enumerate(peers)
+    ]
+    send_when = (None, c < ncol - 1, c > 0, c < ncol - 1, c > 0)
+    recv_when = (None, c > 0, c < ncol - 1, c > 0, c < ncol - 1)
+
+    def guarded(cond, fn):
+        if cond is None:
+            fn()
+        else:
+            pl.when(cond)(fn)
+
+    for cp, cond in zip(out, send_when):
+        guarded(cond, cp.start)
+
+    for i in range(9):
+        kb[i] = jnp.broadcast_to(k_ref[i : i + 1, :].astype(jnp.float32), (span, wide))
+    bb[...] = jnp.broadcast_to(b_ref[...], (span, wide))
+    proj = jnp.dot(x_ref[...].reshape(rows * span, width), w_ref[...],
+                   preferred_element_type=jnp.float32)
+    proj = proj.astype(jnp.bfloat16).astype(jnp.float32)
+    for i in range(rows):
+        pext[pl.ds((1 + i) * pitch + 8, span), :] = proj[i * span : (i + 1) * span]
+    other_row = r * (rows + 1)
+    pext[pl.ds(pl.multiple_of(other_row * pitch, 8), pitch), :] = jnp.zeros((pitch, wide),
+                                                                            jnp.float32)
+
+    for cp, cond in zip(out, send_when):
+        guarded(cond, cp.wait_send)
+    for cp, cond in zip(out, recv_when):
+        guarded(cond, cp.wait_recv)
+
+    hp[...] = jnp.dot(halo[...].reshape(5 * span, width), w_ref[...],
+                      preferred_element_type=jnp.float32).astype(jnp.bfloat16).astype(jnp.float32)
+    halo_row = partner * (rows + 1)
+    base = pl.multiple_of(halo_row * pitch, 8)
+    pext[pl.ds(base + 8, span), :] = hp[0:span, :]
+    pext[pl.ds(base + 7, 1), :] = hp[3 * span : 3 * span + 1, :]
+    pext[pl.ds(base + 8 + span, 1), :] = hp[4 * span : 4 * span + 1, :]
+    for i in range(rows):
+        pext[pl.ds((1 + i) * pitch + 7, 1), :] = hp[pl.ds(span + i, 1), :]
+        pext[pl.ds((1 + i) * pitch + 8 + span, 1), :] = hp[pl.ds(2 * span + i, 1), :]
+
+    def row_body(i, carry):
+        res = []
+        for grp in range(3):
+            lanes = pl.ds(grp * width, width)
+            acc = bb[:, lanes]
+            for a in range(3):
+                window = pext[pl.ds(pl.multiple_of((i + a) * pitch, 8), pitch), lanes]
+                for b in range(3):
+                    acc = acc + window[7 + b : 7 + b + span] * kb[a * 3 + b, :, lanes]
+            res.append(acc.astype(jnp.bfloat16))
+        dst = pl.ds(pl.multiple_of(i * span, 16), span)
+        q_out[dst, :] = res[0]
+        p_out[dst, :] = (res[1].astype(jnp.float32) * res[2].astype(jnp.float32)).astype(
+            jnp.bfloat16)
+        return carry
+
+    lax.fori_loop(0, rows, row_body, 0)
+
+
 def on_device(image_tokens, w_in, conv_kernel, conv_bias, long_filter, skip_gain, w_out):
     row_count, col_count, width = image_tokens.shape
-    tokens = extended(image_tokens, (("row", 0), ("col", 1)), 1)
-    projected = jnp.dot(
-        tokens.reshape(-1, width), w_in, preferred_element_type=jnp.float32
-    ).astype(jnp.bfloat16)
-    projected = projected.reshape(row_count + 2, col_count + 2, 3 * width)
-    mixed = depthwise(projected, conv_kernel, conv_bias, row_count, col_count)
-    query = mixed[:, :, :width]
-    key = mixed[:, :, width : 2 * width].astype(jnp.float32)
-    value = mixed[:, :, 2 * width :].astype(jnp.float32)
-    product = (key * value).astype(jnp.bfloat16)
+    pitch = 48
+    flat = row_count * col_count
+    wide = w_in.shape[1]
+    vmem = pl.BlockSpec(memory_space=pltpu.VMEM)
+    edge = lax.dynamic_index_in_dim(
+        image_tokens, (1 - lax.axis_index("row")) * (row_count - 1), 0, keepdims=False)
+    corner_shape = (col_count, width)
+    send = jnp.stack([
+        edge,
+        image_tokens[:, col_count - 1],
+        image_tokens[:, 0],
+        jnp.broadcast_to(edge[col_count - 1], corner_shape),
+        jnp.broadcast_to(edge[0], corner_shape),
+    ])
+    query, product = pl.pallas_call(
+        functools.partial(front_kernel, row_count, col_count, pitch),
+        out_shape=(
+            jax.ShapeDtypeStruct((flat, width), jnp.bfloat16),
+            jax.ShapeDtypeStruct((flat, width), jnp.bfloat16),
+        ),
+        in_specs=[vmem] * 5,
+        out_specs=(vmem, vmem),
+        scratch_shapes=[
+            pltpu.VMEM((5, col_count, width), jnp.bfloat16),
+            pltpu.VMEM(((row_count + 2) * pitch, wide), jnp.float32),
+            pltpu.VMEM((9, col_count, wide), jnp.float32),
+            pltpu.VMEM((col_count, wide), jnp.float32),
+            pltpu.VMEM((5 * col_count, wide), jnp.float32),
+            pltpu.SemaphoreType.DMA((5,)),
+            pltpu.SemaphoreType.DMA((5,)),
+        ],
+        compiler_params=pltpu.CompilerParams(
+            collective_id=0, has_side_effects=True, vmem_limit_bytes=48 * 1024 * 1024
+        ),
+    )(
+        send,
+        image_tokens,
+        w_in,
+        conv_kernel.reshape(9, wide),
+        conv_bias.reshape(1, wide),
+    )
     count = lax.axis_size("row")
     prev = lax.ppermute(product, "row", [(i, i + 1) for i in range(count - 1)])
-    flat = row_count * col_count
-    vmem = pl.BlockSpec(memory_space=pltpu.VMEM)
     out = pl.pallas_call(
         functools.partial(longconv_kernel, row_count, col_count),
         out_shape=jax.ShapeDtypeStruct((flat, width), jnp.bfloat16),
@@ -93,9 +205,9 @@
             pltpu.VMEM((flat, width), jnp.float32),
         ],
     )(
-        prev.reshape(flat, width),
-        product.reshape(flat, width),
-        query.reshape(flat, width),
+        prev,
+        product,
+        query,
         long_filter,
         skip_gain.reshape(1, width),
         w_out,

time: 42.2 us -> 35.9 us (0.85)
  the two profiles are of different devices: /device:TPU:127 before, /device:TPU:3 now
where the time goes in v2:
time: 35.9 us; the launch traced here: 35.6 us
  Pallas kernels  25.5 us (71%)
  local copies, waits for them, and re-layouts  6.16 us (17%)
  waiting for transfers between devices  2.5 us (7%)
  starting transfers between devices  1.28 us (4%)
    pallas_call x1, Pallas kernels, on_device(): pl.pallas_call(functools.partial(front_kernel, row_count, col_count, pitc...  18.3 us
    pallas_call x1, Pallas kernels, on_device(): pl.pallas_call(functools.partial(longconv_kernel, row_count, col_count),...  7.21 us
    unnamed x18, local copies, waits for them, and re-layouts  4.37 us
    ppermute x1, waiting for transfers between devices, on_device(): prev = lax.ppermute(product, 'row', [(i, i + 1) for i in range(count - 1)])  2.5 us
    ppermute x1, starting transfers between devices, on_device(): prev = lax.ppermute(product, 'row', [(i, i + 1) for i in range(count - 1)])  1.28 us
    slice x1, local copies, waits for them, and re-layouts, on_device(): image_tokens[:, 0]  1.02 us
    slice x1, local copies, waits for them, and re-layouts, on_device(): edge[0]  0.73 us
  transfers between devices with their start and end apart: 1, of which 1 were waited for; matrix products, arithmetic and copies ran while one was open for 0% of the time, Pallas kernels for 0%

profile of v2, /device:TPU:3, one launch (start us, length us, event | category | flops | bytes accessed | tf_op | source)
XLA Modules:
  0.0 35.6 jit_solution(6232423576111444662)
XLA Ops:
  0.0 1.0 %fusion.2 = (bf16[32,1,256]{2,1,0:T(2,128)(2,1)S(1)}, bf16[32,1,256]{2,1,0:T(2,128)(2,1)S(1)}) fusion(bf16[32,32,256]{2,1,0:T(8,128)(2,1)} %x_ref.1), kind=kLoop, calls=%fused_computation.9 | loop fusion | bytes 65536 | tf_op jit(solution)/shard_map/slice | solution.py:163
  1.0 0.0 copy-start.5
  1.0 0.7 %dynamic-slice_dynamic-update-slice_fusion = bf16[5,32,256]{2,1,0:T(8,128)(2,1)S(1)} fusion(bf16[32,32,256]{2,1,0:T(8,128)(2,1)} %x_ref.1, s32[]{:T(128)S(6)} %select_n.4), kind=kLoop, calls=%fused_computation.4 | loop fusion | bytes 32772
  1.8 0.0 copy-start.6
  1.8 0.7 %dynamic-slice_reduce_fusion = (bf16[256]{0:T(256)(128)(2,1)S(1)}, bf16[256]{0:T(256)(128)(2,1)S(1)}) fusion(bf16[32,32,256]{2,1,0:T(8,128)(2,1)} %x_ref.1, s32[]{:T(128)S(6)} %select_n.4, s32[]{:T(128)S(6)} %add.7), kind=kLoop, calls=%fused_computation.7 | loop fusion | bytes 2056 | tf_op jit(solution)/shard_map/slice | solution.py:165
  2.5 0.0 copy-done.6
  2.5 0.0 copy-done.5
  2.6 0.0 copy-start
  2.6 1.0 %copy-done = bf16[32,32,256]{2,1,0:T(8,128)(2,1)S(1)} copy-done((bf16[32,32,256]{2,1,0:T(8,128)(2,1)S(1)}, bf16[32,32,256]{2,1,0:T(8,128)(2,1)}, u32[]{:S(2)}) %copy-start) | copy-done | bytes 524312
  3.7 0.0 copy-start.3
  3.7 1.0 %copy-done.3 = bf16[256,768]{1,0:T(8,128)(2,1)S(1)} copy-done((bf16[256,768]{1,0:T(8,128)(2,1)S(1)}, bf16[256,768]{1,0:T(8,128)(2,1)}, u32[]{:S(2)}) %copy-start.3) | copy-done | bytes 393240
  4.7 18.3 %shard_map.73 = (bf16[1024,256]{1,0:T(8,128)(2,1)S(1)}, bf16[1024,256]{1,0:T(8,128)(2,1)S(1)}) custom-call(bf16[5,32,256]{2,1,0:T(8,128)(2,1)S(1)} %constant_dynamic-update-slice_fusion.send_ref, bf16[32,32,256]{2,1,0:T(8,128)(2,1)S(1)} %copy-done, bf16[256,768]{1,0:T(8,128)(2,1)S(1)} %copy-done.3, bf16[9,768]{1,0:T(8,128)(2,1)S(1)} %reshape.16.k_ref, ...), custom_call_target="tpu_custom_call" | custom-call | tf_op jit(solution)/shard_map/pallas_call | solution.py:167
  23.0 0.0 copy-start.1
  23.0 0.8 %copy-done.1 = bf16[1024,256]{1,0:T(8,128)(2,1)} copy-done((bf16[1024,256]{1,0:T(8,128)(2,1)}, bf16[1024,256]{1,0:T(8,128)(2,1)S(1)}, u32[]{:S(2)}) %copy-start.1) | copy-done | bytes 524312
  23.8 0.0 copy-start.2
  23.8 1.3 %collective-permute-start = (bf16[1024,256]{1,0:T(8,128)(2,1)S(1)}, bf16[1024,256]{1,0:T(8,128)(2,1)S(1)}, u32[]{:S(2)}, u32[]{:S(2)}) collective-permute-start(bf16[1024,256]{1,0:T(8,128)(2,1)S(1)} %get-tuple-element.7.own_ref), channel_id=1, source_target_pairs={{0,128},{1,129},{2,130},{3,131},{4,132},{5,133},{6,134},{7,135},{8... | collective-permute-start | bytes 1572872 | tf_op jit(solution)/shard_map/ppermute | solution.py:195
  25.1 2.5 %collective-permute-done.prev_ref = bf16[1024,256]{1,0:T(8,128)(2,1)S(1)} collective-permute-done((bf16[1024,256]{1,0:T(8,128)(2,1)S(1)}, bf16[1024,256]{1,0:T(8,128)(2,1)S(1)}, u32[]{:S(2)}, u32[]{:S(2)}) %collective-permute-start) | collective-permute-done | bytes 524320 | tf_op jit(solution)/shard_map/ppermute | solution.py:195
  27.6 0.0 copy-start.4
  27.6 0.0 copy-done.2
  27.6 0.8 %copy-done.4 = bf16[1024,256]{1,0:T(8,128)(2,1)} copy-done((bf16[1024,256]{1,0:T(8,128)(2,1)}, bf16[1024,256]{1,0:T(8,128)(2,1)S(1)}, u32[]{:S(2)}) %copy-start.4) | copy-done | bytes 524312
  28.4 7.2 %shard_map.74 = bf16[1024,256]{1,0:T(8,128)(2,1)} custom-call(bf16[1024,256]{1,0:T(8,128)(2,1)} %copy-done.4, bf16[1024,256]{1,0:T(8,128)(2,1)} %copy-done.2, bf16[1024,256]{1,0:T(8,128)(2,1)} %copy-done.1, bf16[64,256]{1,0:T(8,128)(2,1)} %filt_ref.1, f32[1,256]{1,0:T(1,128)} %bitcast.10, bf16[256,256]{1,0:T(8,128)(2,1)} %wout_ref.1), custom_call_target="tpu_custom_call" | custom-call | tf_op jit(solution)/shard_map/pallas_call | solution.py:196
  (6 shorter events, 0.1 us)
Async XLA Ops:
  1.0 1.5 %copy-start.5 = (bf16[3,3,768]{2,1,0:T(4,128)(2,1)S(1)}, bf16[3,3,768]{2,1,0:T(4,128)(2,1)}, u32[]{:S(2)}) copy-start(bf16[3,3,768]{2,1,0:T(4,128)(2,1)} %param.9) | copy-start | bytes 41476
  1.8 0.7 %copy-start.6 = (f32[768]{0:T(1024)S(1)}, f32[768]{0:T(1024)}, u32[]{:S(2)}) copy-start(f32[768]{0:T(1024)} %param.10) | copy-start | bytes 9220
  2.6 1.0 %copy-start = (bf16[32,32,256]{2,1,0:T(8,128)(2,1)S(1)}, bf16[32,32,256]{2,1,0:T(8,128)(2,1)}, u32[]{:S(2)}) copy-start(bf16[32,32,256]{2,1,0:T(8,128)(2,1)} %x_ref.1) | copy-start | bytes 1572868
  3.7 1.0 %copy-start.3 = (bf16[256,768]{1,0:T(8,128)(2,1)S(1)}, bf16[256,768]{1,0:T(8,128)(2,1)}, u32[]{:S(2)}) copy-start(bf16[256,768]{1,0:T(8,128)(2,1)} %w_ref.1) | copy-start | bytes 1179652
  23.0 0.8 %copy-start.1 = (bf16[1024,256]{1,0:T(8,128)(2,1)}, bf16[1024,256]{1,0:T(8,128)(2,1)S(1)}, u32[]{:S(2)}) copy-start(bf16[1024,256]{1,0:T(8,128)(2,1)S(1)} %get-tuple-element.8.q_ref) | copy-start | bytes 1572868
  23.8 3.8 %copy-start.2 = (bf16[1024,256]{1,0:T(8,128)(2,1)}, bf16[1024,256]{1,0:T(8,128)(2,1)S(1)}, u32[]{:S(2)}) copy-start(bf16[1024,256]{1,0:T(8,128)(2,1)S(1)} %get-tuple-element.7.own_ref) | copy-start | bytes 1572868
  23.8 3.8 %collective-permute-start = (bf16[1024,256]{1,0:T(8,128)(2,1)S(1)}, bf16[1024,256]{1,0:T(8,128)(2,1)S(1)}, u32[]{:S(2)}, u32[]{:S(2)}) collective-permute-start(bf16[1024,256]{1,0:T(8,128)(2,1)S(1)} %get-tuple-element.7.own_ref), channel_id=1, source_target_pairs={{0,128},{1,129},{2,130},{3,131},{4,132},{5,133},{6,134},{7,135},{8... | collective-permute-start | bytes 1572872 | tf_op jit(solution)/shard_map/ppermute | solution.py:195
  27.6 0.8 %copy-start.4 = (bf16[1024,256]{1,0:T(8,128)(2,1)}, bf16[1024,256]{1,0:T(8,128)(2,1)S(1)}, u32[]{:S(2)}) copy-start(bf16[1024,256]{1,0:T(8,128)(2,1)S(1)} %collective-permute-done.prev_ref) | copy-start | bytes 1572868

commit v3 on v2

--- a/solution.py
+++ b/solution.py
@@ -66,7 +66,7 @@
 
 
 def front_kernel(rows, span, pitch, send_ref, x_ref, w_ref, k_ref, b_ref, q_out, p_out,
-                 halo, pext, kb, bb, hp, send_sem, recv_sem):
+                 halo, pext, shifted, kb, bb, hp, send_sem, recv_sem):
     width = x_ref.shape[2]
     wide = w_ref.shape[1]
     r = lax.axis_index("row")
@@ -129,15 +129,25 @@
         pext[pl.ds((1 + i) * pitch + 7, 1), :] = hp[pl.ds(span + i, 1), :]
         pext[pl.ds((1 + i) * pitch + 8 + span, 1), :] = hp[pl.ds(2 * span + i, 1), :]
 
+    def shift_body(i, carry):
+        window = pext[pl.ds(pl.multiple_of(i * pitch, 8), pitch), :]
+        dst = pl.ds(pl.multiple_of(i * span, 8), span)
+        shifted[0, dst, :] = window[7 : 7 + span]
+        shifted[1, dst, :] = window[8 : 8 + span]
+        shifted[2, dst, :] = window[9 : 9 + span]
+        return carry
+
+    lax.fori_loop(0, rows + 2, shift_body, 0)
+
     def row_body(i, carry):
         res = []
         for grp in range(3):
             lanes = pl.ds(grp * width, width)
             acc = bb[:, lanes]
             for a in range(3):
-                window = pext[pl.ds(pl.multiple_of((i + a) * pitch, 8), pitch), lanes]
+                src = pl.ds(pl.multiple_of((i + a) * span, 8), span)
                 for b in range(3):
-                    acc = acc + window[7 + b : 7 + b + span] * kb[a * 3 + b, :, lanes]
+                    acc = acc + shifted[b, src, lanes] * kb[a * 3 + b, :, lanes]
             res.append(acc.astype(jnp.bfloat16))
         dst = pl.ds(pl.multiple_of(i * span, 16), span)
         q_out[dst, :] = res[0]
@@ -175,6 +185,7 @@
         scratch_shapes=[
             pltpu.VMEM((5, col_count, width), jnp.bfloat16),
             pltpu.VMEM(((row_count + 2) * pitch, wide), jnp.float32),
+            pltpu.VMEM((3, (row_count + 2) * col_count, wide), jnp.float32),
             pltpu.VMEM((9, col_count, wide), jnp.float32),
             pltpu.VMEM((col_count, wide), jnp.float32),
             pltpu.VMEM((5 * col_count, wide), jnp.float32),

time: 35.9 us -> 34.6 us (0.964)
  Pallas kernels: 25.5 us -> 24.3 us
    pallas_call x1, Pallas kernels: 18.3 us -> 17.1 us  [on_device(): pl.pallas_call(functools.partial(front_kernel, row_count, col_count, pitc...]
where the time goes in v3:
time: 34.6 us; the launch traced here: 34.3 us
  Pallas kernels  24.3 us (70%)
  local copies, waits for them, and re-layouts  6.16 us (18%)
  waiting for transfers between devices  2.5 us (7%)
  starting transfers between devices  1.28 us (4%)
    pallas_call x1, Pallas kernels, on_device(): pl.pallas_call(functools.partial(front_kernel, row_count, col_count, pitc...  17.1 us
    pallas_call x1, Pallas kernels, on_device(): pl.pallas_call(functools.partial(longconv_kernel, row_count, col_count),...  7.19 us
    unnamed x18, local copies, waits for them, and re-layouts  4.37 us
    ppermute x1, waiting for transfers between devices, on_device(): prev = lax.ppermute(product, 'row', [(i, i + 1) for i in range(count - 1)])  2.5 us
    ppermute x1, starting transfers between devices, on_device(): prev = lax.ppermute(product, 'row', [(i, i + 1) for i in range(count - 1)])  1.28 us
    slice x1, local copies, waits for them, and re-layouts, on_device(): image_tokens[:, 0]  1.02 us
    slice x1, local copies, waits for them, and re-layouts, on_device(): edge[0]  0.73 us
  transfers between devices with their start and end apart: 1, of which 1 were waited for; matrix products, arithmetic and copies ran while one was open for 0% of the time, Pallas kernels for 0%

profile of v3, /device:TPU:3, one launch (start us, length us, event | category | flops | bytes accessed | tf_op | source)
XLA Modules:
  0.0 34.3 jit_solution(3922000246166502427)
XLA Ops:
  0.0 1.0 %fusion.2 = (bf16[32,1,256]{2,1,0:T(2,128)(2,1)S(1)}, bf16[32,1,256]{2,1,0:T(2,128)(2,1)S(1)}) fusion(bf16[32,32,256]{2,1,0:T(8,128)(2,1)} %x_ref.1), kind=kLoop, calls=%fused_computation.9 | loop fusion | bytes 65536 | tf_op jit(solution)/shard_map/slice | solution.py:173
  1.0 0.0 copy-start.5
  1.0 0.7 %dynamic-slice_dynamic-update-slice_fusion = bf16[5,32,256]{2,1,0:T(8,128)(2,1)S(1)} fusion(bf16[32,32,256]{2,1,0:T(8,128)(2,1)} %x_ref.1, s32[]{:T(128)S(6)} %select_n.4), kind=kLoop, calls=%fused_computation.4 | loop fusion | bytes 32772
  1.8 0.0 copy-start.6
  1.8 0.7 %dynamic-slice_reduce_fusion = (bf16[256]{0:T(256)(128)(2,1)S(1)}, bf16[256]{0:T(256)(128)(2,1)S(1)}) fusion(bf16[32,32,256]{2,1,0:T(8,128)(2,1)} %x_ref.1, s32[]{:T(128)S(6)} %select_n.4, s32[]{:T(128)S(6)} %add.7), kind=kLoop, calls=%fused_computation.7 | loop fusion | bytes 2056 | tf_op jit(solution)/shard_map/slice | solution.py:175
  2.5 0.0 copy-done.6
  2.5 0.0 copy-done.5
  2.6 0.0 copy-start
  2.6 1.0 %copy-done = bf16[32,32,256]{2,1,0:T(8,128)(2,1)S(1)} copy-done((bf16[32,32,256]{2,1,0:T(8,128)(2,1)S(1)}, bf16[32,32,256]{2,1,0:T(8,128)(2,1)}, u32[]{:S(2)}) %copy-start) | copy-done | bytes 524312
  3.7 0.0 copy-start.3
  3.7 1.0 %copy-done.3 = bf16[256,768]{1,0:T(8,128)(2,1)S(1)} copy-done((bf16[256,768]{1,0:T(8,128)(2,1)S(1)}, bf16[256,768]{1,0:T(8,128)(2,1)}, u32[]{:S(2)}) %copy-start.3) | copy-done | bytes 393240
  4.7 17.1 %shard_map.73 = (bf16[1024,256]{1,0:T(8,128)(2,1)S(1)}, bf16[1024,256]{1,0:T(8,128)(2,1)S(1)}) custom-call(bf16[5,32,256]{2,1,0:T(8,128)(2,1)S(1)} %constant_dynamic-update-slice_fusion.send_ref, bf16[32,32,256]{2,1,0:T(8,128)(2,1)S(1)} %copy-done, bf16[256,768]{1,0:T(8,128)(2,1)S(1)} %copy-done.3, bf16[9,768]{1,0:T(8,128)(2,1)S(1)} %reshape.16.k_ref, ...), custom_call_target="tpu_custom_call" | custom-call | tf_op jit(solution)/shard_map/pallas_call | solution.py:177
  21.7 0.0 copy-start.1
  21.8 0.8 %copy-done.1 = bf16[1024,256]{1,0:T(8,128)(2,1)} copy-done((bf16[1024,256]{1,0:T(8,128)(2,1)}, bf16[1024,256]{1,0:T(8,128)(2,1)S(1)}, u32[]{:S(2)}) %copy-start.1) | copy-done | bytes 524312
  22.6 0.0 copy-start.2
  22.6 1.3 %collective-permute-start = (bf16[1024,256]{1,0:T(8,128)(2,1)S(1)}, bf16[1024,256]{1,0:T(8,128)(2,1)S(1)}, u32[]{:S(2)}, u32[]{:S(2)}) collective-permute-start(bf16[1024,256]{1,0:T(8,128)(2,1)S(1)} %get-tuple-element.7.own_ref), channel_id=1, source_target_pairs={{0,128},{1,129},{2,130},{3,131},{4,132},{5,133},{6,134},{7,135},{8... | collective-permute-start | bytes 1572872 | tf_op jit(solution)/shard_map/ppermute | solution.py:206
  23.8 2.5 %collective-permute-done.prev_ref = bf16[1024,256]{1,0:T(8,128)(2,1)S(1)} collective-permute-done((bf16[1024,256]{1,0:T(8,128)(2,1)S(1)}, bf16[1024,256]{1,0:T(8,128)(2,1)S(1)}, u32[]{:S(2)}, u32[]{:S(2)}) %collective-permute-start) | collective-permute-done | bytes 524320 | tf_op jit(solution)/shard_map/ppermute | solution.py:206
  26.4 0.0 copy-start.4
  26.4 0.0 copy-done.2
  26.4 0.8 %copy-done.4 = bf16[1024,256]{1,0:T(8,128)(2,1)} copy-done((bf16[1024,256]{1,0:T(8,128)(2,1)}, bf16[1024,256]{1,0:T(8,128)(2,1)S(1)}, u32[]{:S(2)}) %copy-start.4) | copy-done | bytes 524312
  27.1 7.2 %shard_map.74 = bf16[1024,256]{1,0:T(8,128)(2,1)} custom-call(bf16[1024,256]{1,0:T(8,128)(2,1)} %copy-done.4, bf16[1024,256]{1,0:T(8,128)(2,1)} %copy-done.2, bf16[1024,256]{1,0:T(8,128)(2,1)} %copy-done.1, bf16[64,256]{1,0:T(8,128)(2,1)} %filt_ref.1, f32[1,256]{1,0:T(1,128)} %bitcast.10, bf16[256,256]{1,0:T(8,128)(2,1)} %wout_ref.1), custom_call_target="tpu_custom_call" | custom-call | tf_op jit(solution)/shard_map/pallas_call | solution.py:207
  (6 shorter events, 0.1 us)
Async XLA Ops:
  1.0 1.5 %copy-start.5 = (bf16[3,3,768]{2,1,0:T(4,128)(2,1)S(1)}, bf16[3,3,768]{2,1,0:T(4,128)(2,1)}, u32[]{:S(2)}) copy-start(bf16[3,3,768]{2,1,0:T(4,128)(2,1)} %param.9) | copy-start | bytes 41476
  1.8 0.7 %copy-start.6 = (f32[768]{0:T(1024)S(1)}, f32[768]{0:T(1024)}, u32[]{:S(2)}) copy-start(f32[768]{0:T(1024)} %param.10) | copy-start | bytes 9220
  2.6 1.0 %copy-start = (bf16[32,32,256]{2,1,0:T(8,128)(2,1)S(1)}, bf16[32,32,256]{2,1,0:T(8,128)(2,1)}, u32[]{:S(2)}) copy-start(bf16[32,32,256]{2,1,0:T(8,128)(2,1)} %x_ref.1) | copy-start | bytes 1572868
  3.7 1.0 %copy-start.3 = (bf16[256,768]{1,0:T(8,128)(2,1)S(1)}, bf16[256,768]{1,0:T(8,128)(2,1)}, u32[]{:S(2)}) copy-start(bf16[256,768]{1,0:T(8,128)(2,1)} %w_ref.1) | copy-start | bytes 1179652
  21.7 0.8 %copy-start.1 = (bf16[1024,256]{1,0:T(8,128)(2,1)}, bf16[1024,256]{1,0:T(8,128)(2,1)S(1)}, u32[]{:S(2)}) copy-start(bf16[1024,256]{1,0:T(8,128)(2,1)S(1)} %get-tuple-element.8.q_ref) | copy-start | bytes 1572868
  22.6 3.8 %copy-start.2 = (bf16[1024,256]{1,0:T(8,128)(2,1)}, bf16[1024,256]{1,0:T(8,128)(2,1)S(1)}, u32[]{:S(2)}) copy-start(bf16[1024,256]{1,0:T(8,128)(2,1)S(1)} %get-tuple-element.7.own_ref) | copy-start | bytes 1572868
  22.6 3.8 %collective-permute-start = (bf16[1024,256]{1,0:T(8,128)(2,1)S(1)}, bf16[1024,256]{1,0:T(8,128)(2,1)S(1)}, u32[]{:S(2)}, u32[]{:S(2)}) collective-permute-start(bf16[1024,256]{1,0:T(8,128)(2,1)S(1)} %get-tuple-element.7.own_ref), channel_id=1, source_target_pairs={{0,128},{1,129},{2,130},{3,131},{4,132},{5,133},{6,134},{7,135},{8... | collective-permute-start | bytes 1572872 | tf_op jit(solution)/shard_map/ppermute | solution.py:206
  26.4 0.8 %copy-start.4 = (bf16[1024,256]{1,0:T(8,128)(2,1)}, bf16[1024,256]{1,0:T(8,128)(2,1)S(1)}, u32[]{:S(2)}) copy-start(bf16[1024,256]{1,0:T(8,128)(2,1)S(1)} %collective-permute-done.prev_ref) | copy-start | bytes 1572868

commit v4 on v1

v4 whole, which is shorter than its diff:
```python
import functools

import jax
import jax.numpy as jnp
from jax import lax
from jax.experimental import pallas as pl
from jax.experimental.pallas import tpu as pltpu
from jax.sharding import PartitionSpec as P


def layer_kernel(rows, span, pitch, x_ref, w_ref, k_ref, b_ref, filt_ref, gain_ref, wout_ref,
                 out_ref, pext, shifted, kb, bb, send_col, recv_col, recv_row, own_b, prev_b,
                 ext, fb, qf, gated, send_sem, recv_sem):
    width = out_ref.shape[1]
    wide = w_ref.shape[1]
    count = rows * span
    r = lax.axis_index("row")
    c = lax.axis_index("col")
    ncol = lax.axis_size("col")
    partner = 1 - r
    edge = partner * (rows - 1)
    mesh_id = pl.DeviceIdType.MESH
    right = lax.rem(c + 1, ncol)
    left = lax.rem(c + ncol - 1, ncol)
    peers = ((r, right), (r, left), (partner, right), (partner, left), (partner, c), (partner, c))

    recv_col[...] = jnp.zeros_like(recv_col)
    barrier = pltpu.get_barrier_semaphore()
    for dev in peers[:5]:
        pl.semaphore_signal(barrier, 1, device_id=dev, device_id_type=mesh_id)

    for i in range(9):
        kb[i] = jnp.broadcast_to(k_ref[i : i + 1, :].astype(jnp.float32), (span, wide))
    bb[...] = jnp.broadcast_to(b_ref[...], (span, wide))
    proj = jnp.dot(x_ref[...], w_ref[...], preferred_element_type=jnp.float32)
    proj = proj.astype(jnp.bfloat16).astype(jnp.float32)
    for i in range(rows):
        pext[pl.ds((1 + i) * pitch + 8, span), :] = proj[i * span : (i + 1) * span]
    other_row = r * (rows + 1)
    pext[pl.ds(pl.multiple_of(other_row * pitch, 8), pitch), :] = jnp.zeros((pitch, wide),
                                                                            jnp.float32)
    for i in range(rows):
        send_col[0, i : i + 1, :] = pext[pl.ds((1 + i) * pitch + 8 + span - 1, 1), :]
        send_col[1, i : i + 1, :] = pext[pl.ds((1 + i) * pitch + 8, 1), :]
    edge_base = pl.multiple_of((1 + edge) * pitch, 8)
    send_col[2, 0:8, :] = jnp.broadcast_to(pext[pl.ds(edge_base + 8 + span - 1, 1), :], (8, wide))
    send_col[3, 0:8, :] = jnp.broadcast_to(pext[pl.ds(edge_base + 8, 1), :], (8, wide))

    pl.semaphore_wait(barrier, 5)
    copies = [
        pltpu.make_async_remote_copy(send_col.at[slot], recv_col.at[slot], send_sem.at[slot],
                                     recv_sem.at[slot], device_id=peers[slot],
                                     device_id_type=mesh_id)
        for slot in range(4)
    ]
    copies.append(pltpu.make_async_remote_copy(
        pext.at[pl.ds(edge_base + 8, span)], recv_row, send_sem.at[4], recv_sem.at[4],
        device_id=peers[4], device_id_type=mesh_id))
    product_copy = pltpu.make_async_remote_copy(
        own_b, prev_b, send_sem.at[5], recv_sem.at[5], device_id=peers[5],
        device_id_type=mesh_id)
    send_when = (c < ncol - 1, c > 0, c < ncol - 1, c > 0, None)
    recv_when = (c > 0, c < ncol - 1, c > 0, c < ncol - 1, None)

    def guarded(cond, fn):
        if cond is None:
            fn()
        else:
            pl.when(cond)(fn)

    for cp, cond in zip(copies, send_when):
        guarded(cond, cp.start)
    for lag in range(2 * rows):
        fb[lag] = jnp.broadcast_to(filt_ref[lag : lag + 1, :].astype(jnp.float32), (8, width))
    for cp, cond in zip(copies, send_when):
        guarded(cond, cp.wait_send)
    for cp, cond in zip(copies, recv_when):
        guarded(cond, cp.wait_recv)

    halo_base = pl.multiple_of(partner * (rows + 1) * pitch, 8)
    pext[pl.ds(halo_base + 8, span), :] = recv_row[...]
    for i in range(rows):
        pext[pl.ds((1 + i) * pitch + 7, 1), :] = recv_col[0, i : i + 1, :]
        pext[pl.ds((1 + i) * pitch + 8 + span, 1), :] = recv_col[1, i : i + 1, :]
    pext[pl.ds(halo_base + 7, 1), :] = recv_col[2, 0:1, :]
    pext[pl.ds(halo_base + 8 + span, 1), :] = recv_col[3, 0:1, :]

    def shift_body(i, carry):
        window = pext[pl.ds(pl.multiple_of(i * pitch, 8), pitch), :]
        dst = pl.ds(pl.multiple_of(i * span, 8), span)
        shifted[0, dst, :] = window[7 : 7 + span]
        shifted[1, dst, :] = window[8 : 8 + span]
        shifted[2, dst, :] = window[9 : 9 + span]
        return carry

    lax.fori_loop(0, rows + 2, shift_body, 0)

    def row_body(i, carry):
        res = []
        for grp in range(3):
            lanes = pl.ds(grp * width, width)
            acc = bb[:, lanes]
            for a in range(3):
                src = pl.ds(pl.multiple_of((i + a) * span, 8), span)
                for b in range(3):
                    acc = acc + shifted[b, src, lanes] * kb[a * 3 + b, :, lanes]
            res.append(acc.astype(jnp.bfloat16).astype(jnp.float32))
        dst = pl.ds(pl.multiple_of(i * span, 16), span)
        qf[dst, :] = res[0]
        prod = (res[1] * res[2]).astype(jnp.bfloat16)
        own_b[dst, :] = prod
        ext[pl.ds(pl.multiple_of(count + i * span, 16), span), :] = prod.astype(jnp.float32)
        return carry

    lax.fori_loop(0, rows, row_body, 0)

    @pl.when(r == 0)
    def _():
        product_copy.start()

    lane_groups = width // 128

    def own_pass(i, carry):
        lanes = pl.ds(pl.multiple_of((i % lane_groups) * 128, 128), 128)
        w0 = pl.multiple_of((i // lane_groups) * 8, 8)
        acc = [None] * rows
        for src in range(rows, 2 * rows):
            x = ext[pl.ds(src * span + w0, 8), lanes]
            for a in range(src - rows, rows):
                term = fb[rows + a - src, :, lanes] * x
                acc[a] = term if acc[a] is None else acc[a] + term
        for a in range(rows):
            gated[pl.ds(a * span + w0, 8), lanes] = acc[a]
        return carry

    lax.fori_loop(0, (span // 8) * lane_groups, own_pass, 0)

    @pl.when(r == 0)
    def _():
        product_copy.wait_send()
        ext[0:count, :] = jnp.zeros((count, width), jnp.float32)

    @pl.when(r == 1)
    def _():
        product_copy.wait_recv()
        ext[0:count, :] = prev_b[...].astype(jnp.float32)

    def prev_pass(i, carry):
        lanes = pl.ds(pl.multiple_of((i % lane_groups) * 128, 128), 128)
        w0 = pl.multiple_of((i // lane_groups) * 8, 8)
        acc = [gated[pl.ds(a * span + w0, 8), lanes] for a in range(rows)]
        for src in range(rows):
            x = ext[pl.ds(src * span + w0, 8), lanes]
            for a in range(rows):
                acc[a] = acc[a] + fb[rows + a - src, :, lanes] * x
        gain = jnp.broadcast_to(gain_ref[:, lanes], (8, 128))
        for a in range(rows):
            own = ext[pl.ds(count + a * span + w0, 8), lanes]
            q = qf[pl.ds(a * span + w0, 8), lanes]
            gated[pl.ds(a * span + w0, 8), lanes] = q * (acc[a] + gain * own)
        return carry

    lax.fori_loop(0, (span // 8) * lane_groups, prev_pass, 0)
    out_ref[...] = jnp.dot(
        gated[...].astype(jnp.bfloat16), wout_ref[...], preferred_element_type=jnp.float32
    ).astype(out_ref.dtype)


def on_device(image_tokens, w_in, conv_kernel, conv_bias, long_filter, skip_gain, w_out):
    row_count, col_count, width = image_tokens.shape
    pitch = 48
    flat = row_count * col_count
    wide = w_in.shape[1]
    vmem = pl.BlockSpec(memory_space=pltpu.VMEM)
    out = pl.pallas_call(
        functools.partial(layer_kernel, row_count, col_count, pitch),
        out_shape=jax.ShapeDtypeStruct((flat, width), jnp.bfloat16),
        in_specs=[vmem] * 7,
        out_specs=vmem,
        scratch_shapes=[
            pltpu.VMEM(((row_count + 2) * pitch, wide), jnp.float32),
            pltpu.VMEM((3, (row_count + 2) * col_count, wide), jnp.float32),
            pltpu.VMEM((9, col_count, wide), jnp.float32),
            pltpu.VMEM((col_count, wide), jnp.float32),
            pltpu.VMEM((4, row_count, wide), jnp.float32),
            pltpu.VMEM((4, row_count, wide), jnp.float32),
            pltpu.VMEM((col_count, wide), jnp.float32),
            pltpu.VMEM((flat, width), jnp.bfloat16),
            pltpu.VMEM((flat, width), jnp.bfloat16),
            pltpu.VMEM((2 * flat, width), jnp.float32),
            pltpu.VMEM((2 * row_count, 8, width), jnp.float32),
            pltpu.VMEM((flat, width), jnp.float32),
            pltpu.VMEM((flat, width), jnp.float32),
            pltpu.SemaphoreType.DMA((6,)),
            pltpu.SemaphoreType.DMA((6,)),
        ],
        compiler_params=pltpu.CompilerParams(
            collective_id=0, has_side_effects=True, vmem_limit_bytes=48 * 1024 * 1024
        ),
    )(
        image_tokens.reshape(flat, width),
        w_in,
        conv_kernel.reshape(9, wide),
        conv_bias.reshape(1, wide),
        long_filter,
        skip_gain.reshape(1, width),
        w_out,
    )
    return out.reshape(row_count, col_count, width)


def solution(mesh):
    in_specs = (P("row", "col", None), P(), P(), P(), P(), P(), P())
    out_specs = P("row", "col", None)
    return jax.shard_map(
        on_device, mesh=mesh, in_specs=in_specs, out_specs=out_specs, check_vma=False
    )
```

time: 42.2 us -> 31.5 us (0.75)
  the two profiles are of different devices: /device:TPU:127 before, /device:TPU:1 now
where the time goes in v4:
time: 31.5 us; the launch traced here: 31.2 us
  Pallas kernels  26 us (83%)
  local copies, waits for them, and re-layouts  5.19 us (16%)
    pallas_call x1, Pallas kernels, on_device(): pl.pallas_call(functools.partial(layer_kernel, row_count, col_count, pitc...  26 us
    unnamed x11, local copies, waits for them, and re-layouts  3.74 us
    reshape x1, local copies, waits for them, and re-layouts, on_device(): conv_kernel.reshape(9, wide)  0.76 us
    reshape x1, local copies, waits for them, and re-layouts, on_device(): conv_bias.reshape(1, wide)  0.7 us

profile of v4, /device:TPU:1, one launch (start us, length us, event | category | flops | bytes accessed | tf_op | source)
XLA Modules:
  0.0 31.2 jit_solution(1318308765580727045)
XLA Ops:
  0.0 0.0 copy-start.3
  0.0 0.7 %reshape.17.b_ref = f32[1,768]{1,0:T(1,128)S(1)} reshape(f32[768]{0:T(1024)} %param.10) | data formatting | bytes 6144 | tf_op jit(solution)/shard_map/reshape | solution.py:204
  0.7 0.0 copy-start.4
  0.7 0.8 %reshape.16.k_ref = bf16[9,768]{1,0:T(8,128)(2,1)S(1)} reshape(bf16[3,3,768]{2,1,0:T(4,128)(2,1)} %param.9) | data formatting | bytes 27648 | tf_op jit(solution)/shard_map/reshape | solution.py:203
  1.5 0.0 copy-done.3
  1.5 0.0 copy-done.4
  1.5 0.0 copy-start
  1.5 1.0 %copy-done = bf16[32,32,256]{2,1,0:T(8,128)(2,1)S(1)} copy-done((bf16[32,32,256]{2,1,0:T(8,128)(2,1)S(1)}, bf16[32,32,256]{2,1,0:T(8,128)(2,1)}, u32[]{:S(2)}) %copy-start) | copy-done | bytes 524312
  2.5 0.0 copy-start.1
  2.5 1.0 %copy-done.1 = bf16[256,768]{1,0:T(8,128)(2,1)S(1)} copy-done((bf16[256,768]{1,0:T(8,128)(2,1)S(1)}, bf16[256,768]{1,0:T(8,128)(2,1)}, u32[]{:S(2)}) %copy-start.1) | copy-done | bytes 393240
  3.5 0.0 copy-start.2
  3.5 0.9 %copy-done.2 = bf16[256,256]{1,0:T(8,128)(2,1)S(1)} copy-done((bf16[256,256]{1,0:T(8,128)(2,1)S(1)}, bf16[256,256]{1,0:T(8,128)(2,1)}, u32[]{:S(2)}) %copy-start.2) | copy-done | bytes 131096
  4.4 26.0 %shard_map.73 = bf16[1024,256]{1,0:T(8,128)(2,1)S(1)} custom-call(bf16[1024,256]{1,0:T(8,128)(2,1)S(1)} %bitcast.4, bf16[256,768]{1,0:T(8,128)(2,1)S(1)} %copy-done.1, bf16[9,768]{1,0:T(8,128)(2,1)S(1)} %reshape.16.k_ref, f32[1,768]{1,0:T(1,128)S(1)} %reshape.17.b_ref, bf16[64,256]{1,0:T(8,128)(2,1)S(1)} %copy-done.3, f32[1,256]{1,0:T(1,128)S(1)} %bitcast.5, ...), custom_call_target="tpu_custom_call" | custom-call | tf_op jit(solution)/shard_map/pallas_call | solution.py:175
  30.4 0.8 %copy.9 = bf16[32,32,256]{2,1,0:T(8,128)(2,1)} copy(bf16[32,32,256]{2,1,0:T(8,128)(2,1)S(1)} %bitcast.3) | data formatting | bytes 1048576
Async XLA Ops:
  0.0 1.5 %copy-start.3 = (bf16[64,256]{1,0:T(8,128)(2,1)S(1)}, bf16[64,256]{1,0:T(8,128)(2,1)}, u32[]{:S(2)}) copy-start(bf16[64,256]{1,0:T(8,128)(2,1)} %filt_ref.1) | copy-start | bytes 98308
  0.7 0.8 %copy-start.4 = (f32[256]{0:T(256)S(1)}, f32[256]{0:T(256)}, u32[]{:S(2)}) copy-start(f32[256]{0:T(256)} %param.12) | copy-start | bytes 3076
  1.5 1.0 %copy-start = (bf16[32,32,256]{2,1,0:T(8,128)(2,1)S(1)}, bf16[32,32,256]{2,1,0:T(8,128)(2,1)}, u32[]{:S(2)}) copy-start(bf16[32,32,256]{2,1,0:T(8,128)(2,1)} %param.7) | copy-start | bytes 1572868
  2.5 1.0 %copy-start.1 = (bf16[256,768]{1,0:T(8,128)(2,1)S(1)}, bf16[256,768]{1,0:T(8,128)(2,1)}, u32[]{:S(2)}) copy-start(bf16[256,768]{1,0:T(8,128)(2,1)} %w_ref.1) | copy-start | bytes 1179652
  3.5 0.9 %copy-start.2 = (bf16[256,256]{1,0:T(8,128)(2,1)S(1)}, bf16[256,256]{1,0:T(8,128)(2,1)}, u32[]{:S(2)}) copy-start(bf16[256,256]{1,0:T(8,128)(2,1)} %wout_ref.1) | copy-start | bytes 393220

commit v5 on v4

--- a/solution.py
+++ b/solution.py
@@ -26,8 +26,14 @@
 
     recv_col[...] = jnp.zeros_like(recv_col)
     barrier = pltpu.get_barrier_semaphore()
-    for dev in peers[:5]:
-        pl.semaphore_signal(barrier, 1, device_id=dev, device_id_type=mesh_id)
+    conds = (c < ncol - 1, c > 0, c < ncol - 1, c > 0)
+    for dev, cond in zip(peers[:4], conds):
+        @pl.when(cond)
+        def _():
+            pl.semaphore_signal(barrier, 1, device_id=dev, device_id_type=mesh_id)
+    pl.semaphore_signal(barrier, 1, device_id=peers[4], device_id_type=mesh_id)
+    has_left = (c + ncol - 1) // ncol
+    has_right = (2 * ncol - 3 - c) // (ncol - 1)
 
     for i in range(9):
         kb[i] = jnp.broadcast_to(k_ref[i : i + 1, :].astype(jnp.float32), (span, wide))
@@ -46,7 +52,7 @@
     send_col[2, 0:8, :] = jnp.broadcast_to(pext[pl.ds(edge_base + 8 + span - 1, 1), :], (8, wide))
     send_col[3, 0:8, :] = jnp.broadcast_to(pext[pl.ds(edge_base + 8, 1), :], (8, wide))
 
-    pl.semaphore_wait(barrier, 5)
+    pl.semaphore_wait(barrier, 1 + 2 * has_left + 2 * has_right)
     copies = [
         pltpu.make_async_remote_copy(send_col.at[slot], recv_col.at[slot], send_sem.at[slot],
                                      recv_sem.at[slot], device_id=peers[slot],

time: 31.5 us -> 27.6 us (0.88)
  the two profiles are of different devices: /device:TPU:1 before, /device:TPU:129 now
where the time goes in v5:
time: 27.6 us; the launch traced here: 27.3 us
  Pallas kernels  22.1 us (80%)
  local copies, waits for them, and re-layouts  5.19 us (19%)
    pallas_call x1, Pallas kernels, on_device(): pl.pallas_call(functools.partial(layer_kernel, row_count, col_count, pitc...  22.1 us
    unnamed x11, local copies, waits for them, and re-layouts  3.74 us
    reshape x1, local copies, waits for them, and re-layouts, on_device(): conv_kernel.reshape(9, wide)  0.76 us
    reshape x1, local copies, waits for them, and re-layouts, on_device(): conv_bias.reshape(1, wide)  0.7 us

profile of v5, /device:TPU:129, one launch (start us, length us, event | category | flops | bytes accessed | tf_op | source)
XLA Modules:
  0.0 27.3 jit_solution(8334515881678687260)
XLA Ops:
  0.0 0.0 copy-start.3
  0.0 0.7 %reshape.17.b_ref = f32[1,768]{1,0:T(1,128)S(1)} reshape(f32[768]{0:T(1024)} %param.10) | data formatting | bytes 6144 | tf_op jit(solution)/shard_map/reshape | solution.py:210
  0.7 0.0 copy-start.4
  0.7 0.8 %reshape.16.k_ref = bf16[9,768]{1,0:T(8,128)(2,1)S(1)} reshape(bf16[3,3,768]{2,1,0:T(4,128)(2,1)} %param.9) | data formatting | bytes 27648 | tf_op jit(solution)/shard_map/reshape | solution.py:209
  1.5 0.0 copy-done.3
  1.5 0.0 copy-done.4
  1.5 0.0 copy-start
  1.5 1.0 %copy-done = bf16[32,32,256]{2,1,0:T(8,128)(2,1)S(1)} copy-done((bf16[32,32,256]{2,1,0:T(8,128)(2,1)S(1)}, bf16[32,32,256]{2,1,0:T(8,128)(2,1)}, u32[]{:S(2)}) %copy-start) | copy-done | bytes 524312
  2.5 0.0 copy-start.1
  2.5 1.0 %copy-done.1 = bf16[256,768]{1,0:T(8,128)(2,1)S(1)} copy-done((bf16[256,768]{1,0:T(8,128)(2,1)S(1)}, bf16[256,768]{1,0:T(8,128)(2,1)}, u32[]{:S(2)}) %copy-start.1) | copy-done | bytes 393240
  3.5 0.0 copy-start.2
  3.5 0.9 %copy-done.2 = bf16[256,256]{1,0:T(8,128)(2,1)S(1)} copy-done((bf16[256,256]{1,0:T(8,128)(2,1)S(1)}, bf16[256,256]{1,0:T(8,128)(2,1)}, u32[]{:S(2)}) %copy-start.2) | copy-done | bytes 131096
  4.4 22.1 %shard_map.73 = bf16[1024,256]{1,0:T(8,128)(2,1)S(1)} custom-call(bf16[1024,256]{1,0:T(8,128)(2,1)S(1)} %bitcast.4, bf16[256,768]{1,0:T(8,128)(2,1)S(1)} %copy-done.1, bf16[9,768]{1,0:T(8,128)(2,1)S(1)} %reshape.16.k_ref, f32[1,768]{1,0:T(1,128)S(1)} %reshape.17.b_ref, bf16[64,256]{1,0:T(8,128)(2,1)S(1)} %copy-done.3, f32[1,256]{1,0:T(1,128)S(1)} %bitcast.5, ...), custom_call_target="tpu_custom_call" | custom-call | tf_op jit(solution)/shard_map/pallas_call | solution.py:181
  26.5 0.8 %copy.9 = bf16[32,32,256]{2,1,0:T(8,128)(2,1)} copy(bf16[32,32,256]{2,1,0:T(8,128)(2,1)S(1)} %bitcast.3) | data formatting | bytes 1048576
Async XLA Ops:
  0.0 1.5 %copy-start.3 = (bf16[64,256]{1,0:T(8,128)(2,1)S(1)}, bf16[64,256]{1,0:T(8,128)(2,1)}, u32[]{:S(2)}) copy-start(bf16[64,256]{1,0:T(8,128)(2,1)} %filt_ref.1) | copy-start | bytes 98308
  0.7 0.8 %copy-start.4 = (f32[256]{0:T(256)S(1)}, f32[256]{0:T(256)}, u32[]{:S(2)}) copy-start(f32[256]{0:T(256)} %param.12) | copy-start | bytes 3076
  1.5 1.0 %copy-start = (bf16[32,32,256]{2,1,0:T(8,128)(2,1)S(1)}, bf16[32,32,256]{2,1,0:T(8,128)(2,1)}, u32[]{:S(2)}) copy-start(bf16[32,32,256]{2,1,0:T(8,128)(2,1)} %param.7) | copy-start | bytes 1572868
  2.5 1.0 %copy-start.1 = (bf16[256,768]{1,0:T(8,128)(2,1)S(1)}, bf16[256,768]{1,0:T(8,128)(2,1)}, u32[]{:S(2)}) copy-start(bf16[256,768]{1,0:T(8,128)(2,1)} %w_ref.1) | copy-start | bytes 1179652
  3.5 0.9 %copy-start.2 = (bf16[256,256]{1,0:T(8,128)(2,1)S(1)}, bf16[256,256]{1,0:T(8,128)(2,1)}, u32[]{:S(2)}) copy-start(bf16[256,256]{1,0:T(8,128)(2,1)} %wout_ref.1) | copy-start | bytes 393220

commit v6 on v5

--- a/solution.py
+++ b/solution.py
@@ -8,8 +8,8 @@
 from jax.sharding import PartitionSpec as P
 
 
-def layer_kernel(rows, span, pitch, x_ref, w_ref, k_ref, b_ref, filt_ref, gain_ref, wout_ref,
-                 out_ref, pext, shifted, kb, bb, send_col, recv_col, recv_row, own_b, prev_b,
+def layer_kernel(rows, span, pitch, x_hbm, w_hbm, k_hbm, b_hbm, filt_hbm, gain_hbm, wout_hbm,
+                 out_ref, x_ref, w_ref, k_ref, b_ref, filt_ref, gain_ref, wout_ref, load_sem, pext, shifted, kb, bb, send_col, recv_col, recv_row, own_b, prev_b,
                  ext, fb, qf, gated, send_sem, recv_sem):
     width = out_ref.shape[1]
     wide = w_ref.shape[1]
@@ -35,9 +35,20 @@
     has_left = (c + ncol - 1) // ncol
     has_right = (2 * ncol - 3 - c) // (ncol - 1)
 
+    loads = [
+        pltpu.make_async_copy(src, dst, load_sem.at[i])
+        for i, (src, dst) in enumerate((
+            (x_hbm, x_ref), (w_hbm, w_ref), (k_hbm, k_ref), (b_hbm, b_ref),
+            (filt_hbm, filt_ref), (gain_hbm, gain_ref), (wout_hbm, wout_ref)))
+    ]
+    for cp in loads:
+        cp.start()
+    for cp in loads[:4]:
+        cp.wait()
     for i in range(9):
-        kb[i] = jnp.broadcast_to(k_ref[i : i + 1, :].astype(jnp.float32), (span, wide))
-    bb[...] = jnp.broadcast_to(b_ref[...], (span, wide))
+        kb[i] = jnp.broadcast_to(
+            k_ref[i // 3, i % 3 : i % 3 + 1, :].astype(jnp.float32), (span, wide))
+    bb[...] = jnp.broadcast_to(b_ref[...].reshape(1, wide), (span, wide))
     proj = jnp.dot(x_ref[...], w_ref[...], preferred_element_type=jnp.float32)
     proj = proj.astype(jnp.bfloat16).astype(jnp.float32)
     for i in range(rows):
@@ -76,6 +87,8 @@
 
     for cp, cond in zip(copies, send_when):
         guarded(cond, cp.start)
+    for cp in loads[4:]:
+        cp.wait()
     for lag in range(2 * rows):
         fb[lag] = jnp.broadcast_to(filt_ref[lag : lag + 1, :].astype(jnp.float32), (8, width))
     for cp, cond in zip(copies, send_when):
@@ -159,7 +172,7 @@
             x = ext[pl.ds(src * span + w0, 8), lanes]
             for a in range(rows):
                 acc[a] = acc[a] + fb[rows + a - src, :, lanes] * x
-        gain = jnp.broadcast_to(gain_ref[:, lanes], (8, 128))
+        gain = jnp.broadcast_to(gain_ref[lanes].reshape(1, 128), (8, 128))
         for a in range(rows):
             own = ext[pl.ds(count + a * span + w0, 8), lanes]
             q = qf[pl.ds(a * span + w0, 8), lanes]
@@ -181,9 +194,17 @@
     out = pl.pallas_call(
         functools.partial(layer_kernel, row_count, col_count, pitch),
         out_shape=jax.ShapeDtypeStruct((flat, width), jnp.bfloat16),
-        in_specs=[vmem] * 7,
+        in_specs=[pl.BlockSpec(memory_space=pl.ANY)] * 7,
         out_specs=vmem,
         scratch_shapes=[
+            pltpu.VMEM((flat, width), jnp.bfloat16),
+            pltpu.VMEM(w_in.shape, jnp.bfloat16),
+            pltpu.VMEM(conv_kernel.shape, jnp.bfloat16),
+            pltpu.VMEM(conv_bias.shape, jnp.float32),
+            pltpu.VMEM(long_filter.shape, jnp.bfloat16),
+            pltpu.VMEM(skip_gain.shape, jnp.float32),
+            pltpu.VMEM(w_out.shape, jnp.bfloat16),
+            pltpu.SemaphoreType.DMA((7,)),
             pltpu.VMEM(((row_count + 2) * pitch, wide), jnp.float32),
             pltpu.VMEM((3, (row_count + 2) * col_count, wide), jnp.float32),
             pltpu.VMEM((9, col_count, wide), jnp.float32),
@@ -201,15 +222,15 @@
             pltpu.SemaphoreType.DMA((6,)),
         ],
         compiler_params=pltpu.CompilerParams(
-            collective_id=0, has_side_effects=True, vmem_limit_bytes=48 * 1024 * 1024
+            collective_id=0, has_side_effects=True, vmem_limit_bytes=67043328
         ),
     )(
         image_tokens.reshape(flat, width),
         w_in,
-        conv_kernel.reshape(9, wide),
-        conv_bias.reshape(1, wide),
+        conv_kernel,
+        conv_bias,
         long_filter,
-        skip_gain.reshape(1, width),
+        skip_gain,
         w_out,
     )
     return out.reshape(row_count, col_count, width)

time: 27.6 us -> 26.4 us (0.957)
  the two profiles are of different devices: /device:TPU:129 before, /device:TPU:161 now
where the time goes in v6:
time: 26.4 us; the launch traced here: 25.9 us
  Pallas kernels  24 us (91%)
  local copies, waits for them, and re-layouts  1.87 us (7%)
    pallas_call x1, Pallas kernels, on_device(): pl.pallas_call(functools.partial(layer_kernel, row_count, col_count, pitc...  24 us
    unnamed x1, local copies, waits for them, and re-layouts  1.87 us

profile of v6, /device:TPU:161, one launch (start us, length us, event | category | flops | bytes accessed | tf_op | source)
XLA Modules:
  0.0 25.9 jit_solution(4948900211951732253)
XLA Ops:
  0.0 24.0 %shard_map.73 = bf16[1024,256]{1,0:T(8,128)(2,1)} custom-call(bf16[1024,256]{1,0:T(8,128)(2,1)} %bitcast.3, bf16[256,768]{1,0:T(8,128)(2,1)} %w_hbm.1, bf16[3,3,768]{2,1,0:T(4,128)(2,1)} %k_hbm.1, f32[768]{0:T(1024)} %b_hbm.1, bf16[64,256]{1,0:T(8,128)(2,1)} %filt_hbm.1, f32[256]{0:T(256)} %gain_hbm.1, bf16[256,256]{1,0:T(8,128)(2,1)} %wout_hbm.1), custom_call_target="tpu_custom_call" | custom-call | tf_op jit(solution)/shard_map/pallas_call | solution.py:194
  24.0 1.9 %copy.9 = bf16[32,32,256]{2,1,0:T(8,128)(2,1)} copy(bf16[32,32,256]{2,1,0:T(8,128)(2,1)} %bitcast.2) | data formatting | bytes 1048576

commit v7 on v6

--- a/solution.py
+++ b/solution.py
@@ -73,9 +73,14 @@
     copies.append(pltpu.make_async_remote_copy(
         pext.at[pl.ds(edge_base + 8, span)], recv_row, send_sem.at[4], recv_sem.at[4],
         device_id=peers[4], device_id_type=mesh_id))
-    product_copy = pltpu.make_async_remote_copy(
-        own_b, prev_b, send_sem.at[5], recv_sem.at[5], device_id=peers[5],
-        device_id_type=mesh_id)
+    piece = 8 * span
+    pieces = rows // 8
+
+    def product_copy(k):
+        return pltpu.make_async_remote_copy(
+            own_b.at[pl.ds(k * piece, piece)], prev_b.at[pl.ds(k * piece, piece)],
+            send_sem.at[5 + k], recv_sem.at[5 + k], device_id=peers[5],
+            device_id_type=mesh_id)
     send_when = (c < ncol - 1, c > 0, c < ncol - 1, c > 0, None)
     recv_when = (c > 0, c < ncol - 1, c > 0, c < ncol - 1, None)
 
@@ -115,6 +120,10 @@
     lax.fori_loop(0, rows + 2, shift_body, 0)
 
     def row_body(i, carry):
+        @pl.when(jnp.logical_and(r == 0, jnp.logical_and(i > 0, i % 8 == 0)))
+        def _():
+            product_copy(i // 8 - 1).start()
+
         res = []
         for grp in range(3):
             lanes = pl.ds(grp * width, width)
@@ -135,7 +144,7 @@
 
     @pl.when(r == 0)
     def _():
-        product_copy.start()
+        product_copy(pieces - 1).start()
 
     lane_groups = width // 128
 
@@ -156,12 +165,14 @@
 
     @pl.when(r == 0)
     def _():
-        product_copy.wait_send()
+        for k in range(pieces):
+            product_copy(k).wait_send()
         ext[0:count, :] = jnp.zeros((count, width), jnp.float32)
 
     @pl.when(r == 1)
     def _():
-        product_copy.wait_recv()
+        for k in range(pieces):
+            product_copy(k).wait_recv()
         ext[0:count, :] = prev_b[...].astype(jnp.float32)
 
     def prev_pass(i, carry):
@@ -218,8 +229,8 @@
             pltpu.VMEM((2 * row_count, 8, width), jnp.float32),
             pltpu.VMEM((flat, width), jnp.float32),
             pltpu.VMEM((flat, width), jnp.float32),
-            pltpu.SemaphoreType.DMA((6,)),
-            pltpu.SemaphoreType.DMA((6,)),
+            pltpu.SemaphoreType.DMA((5 + row_count // 8,)),
+            pltpu.SemaphoreType.DMA((5 + row_count // 8,)),
         ],
         compiler_params=pltpu.CompilerParams(
             collective_id=0, has_side_effects=True, vmem_limit_bytes=67043328

time: 26.4 us -> 26.1 us (0.989); the launches traced: 25.9 us -> 25.9 us
  no operation moved by 1% of the time
where the time goes in v7:
time: 26.1 us; the launch traced here: 25.9 us
  Pallas kernels  24 us (92%)
  local copies, waits for them, and re-layouts  1.87 us (7%)
    pallas_call x1, Pallas kernels, on_device(): pl.pallas_call(functools.partial(layer_kernel, row_count, col_count, pitc...  24 us
    unnamed x1, local copies, waits for them, and re-layouts  1.87 us

profile of v7, /device:TPU:161, one launch (start us, length us, event | category | flops | bytes accessed | tf_op | source)
XLA Modules:
  0.0 25.9 jit_solution(1878670845976166032)
XLA Ops:
  0.0 24.0 %shard_map.73 = bf16[1024,256]{1,0:T(8,128)(2,1)} custom-call(bf16[1024,256]{1,0:T(8,128)(2,1)} %bitcast.3, bf16[256,768]{1,0:T(8,128)(2,1)} %w_hbm.1, bf16[3,3,768]{2,1,0:T(4,128)(2,1)} %k_hbm.1, f32[768]{0:T(1024)} %b_hbm.1, bf16[64,256]{1,0:T(8,128)(2,1)} %filt_hbm.1, f32[256]{0:T(256)} %gain_hbm.1, bf16[256,256]{1,0:T(8,128)(2,1)} %wout_hbm.1), custom_call_target="tpu_custom_call" | custom-call | tf_op jit(solution)/shard_map/pallas_call | solution.py:205
  24.0 1.9 %copy.9 = bf16[32,32,256]{2,1,0:T(8,128)(2,1)} copy(bf16[32,32,256]{2,1,0:T(8,128)(2,1)} %bitcast.2) | data formatting | bytes 1048576

commit v8 on v7

--- a/solution.py
+++ b/solution.py
@@ -9,8 +9,9 @@
 
 
 def layer_kernel(rows, span, pitch, x_hbm, w_hbm, k_hbm, b_hbm, filt_hbm, gain_hbm, wout_hbm,
-                 out_ref, x_ref, w_ref, k_ref, b_ref, filt_ref, gain_ref, wout_ref, load_sem, pext, shifted, kb, bb, send_col, recv_col, recv_row, own_b, prev_b,
-                 ext, fb, qf, gated, send_sem, recv_sem):
+                 out_ref, x_ref, w_ref, k_ref, b_ref, filt_ref, gain_ref, wout_ref, load_sem, pext,
+                 shifted, kb, bb, send_col, recv_col, recv_row, own_b, prev_b, stage, send_row,
+                 send_cor, recv_cor, ext, fb, qf, gated, send_sem, recv_sem):
     width = out_ref.shape[1]
     wide = w_ref.shape[1]
     count = rows * span
@@ -25,6 +26,7 @@
     peers = ((r, right), (r, left), (partner, right), (partner, left), (partner, c), (partner, c))
 
     recv_col[...] = jnp.zeros_like(recv_col)
+    recv_cor[...] = jnp.zeros_like(recv_cor)
     barrier = pltpu.get_barrier_semaphore()
     conds = (c < ncol - 1, c > 0, c < ncol - 1, c > 0)
     for dev, cond in zip(peers[:4], conds):
@@ -57,22 +59,27 @@
     pext[pl.ds(pl.multiple_of(other_row * pitch, 8), pitch), :] = jnp.zeros((pitch, wide),
                                                                             jnp.float32)
     for i in range(rows):
-        send_col[0, i : i + 1, :] = pext[pl.ds((1 + i) * pitch + 8 + span - 1, 1), :]
-        send_col[1, i : i + 1, :] = pext[pl.ds((1 + i) * pitch + 8, 1), :]
+        stage[0, i : i + 1, :] = pext[pl.ds((1 + i) * pitch + 8 + span - 1, 1), :]
+        stage[1, i : i + 1, :] = pext[pl.ds((1 + i) * pitch + 8, 1), :]
+    send_col[0] = stage[0].astype(jnp.bfloat16)
+    send_col[1] = stage[1].astype(jnp.bfloat16)
     edge_base = pl.multiple_of((1 + edge) * pitch, 8)
-    send_col[2, 0:8, :] = jnp.broadcast_to(pext[pl.ds(edge_base + 8 + span - 1, 1), :], (8, wide))
-    send_col[3, 0:8, :] = jnp.broadcast_to(pext[pl.ds(edge_base + 8, 1), :], (8, wide))
+    send_row[...] = pext[pl.ds(edge_base + 8, span), :].astype(jnp.bfloat16)
+    corner_rows = send_cor.shape[1]
+    send_cor[0] = jnp.broadcast_to(pext[pl.ds(edge_base + 8 + span - 1, 1), :],
+                                   (corner_rows, wide)).astype(jnp.bfloat16)
+    send_cor[1] = jnp.broadcast_to(pext[pl.ds(edge_base + 8, 1), :],
+                                   (corner_rows, wide)).astype(jnp.bfloat16)
 
     pl.semaphore_wait(barrier, 1 + 2 * has_left + 2 * has_right)
+    pairs = ((send_col.at[0], recv_col.at[0]), (send_col.at[1], recv_col.at[1]),
+             (send_cor.at[0], recv_cor.at[0]), (send_cor.at[1], recv_cor.at[1]),
+             (send_row, recv_row))
     copies = [
-        pltpu.make_async_remote_copy(send_col.at[slot], recv_col.at[slot], send_sem.at[slot],
-                                     recv_sem.at[slot], device_id=peers[slot],
-                                     device_id_type=mesh_id)
-        for slot in range(4)
+        pltpu.make_async_remote_copy(src_ref, dst_ref, send_sem.at[slot], recv_sem.at[slot],
+                                     device_id=peers[slot], device_id_type=mesh_id)
+        for slot, (src_ref, dst_ref) in enumerate(pairs)
     ]
-    copies.append(pltpu.make_async_remote_copy(
-        pext.at[pl.ds(edge_base + 8, span)], recv_row, send_sem.at[4], recv_sem.at[4],
-        device_id=peers[4], device_id_type=mesh_id))
     piece = 8 * span
     pieces = rows // 8
 
@@ -102,12 +109,14 @@
         guarded(cond, cp.wait_recv)
 
     halo_base = pl.multiple_of(partner * (rows + 1) * pitch, 8)
-    pext[pl.ds(halo_base + 8, span), :] = recv_row[...]
+    pext[pl.ds(halo_base + 8, span), :] = recv_row[...].astype(jnp.float32)
+    stage[0] = recv_col[0].astype(jnp.float32)
+    stage[1] = recv_col[1].astype(jnp.float32)
     for i in range(rows):
-        pext[pl.ds((1 + i) * pitch + 7, 1), :] = recv_col[0, i : i + 1, :]
-        pext[pl.ds((1 + i) * pitch + 8 + span, 1), :] = recv_col[1, i : i + 1, :]
-    pext[pl.ds(halo_base + 7, 1), :] = recv_col[2, 0:1, :]
-    pext[pl.ds(halo_base + 8 + span, 1), :] = recv_col[3, 0:1, :]
+        pext[pl.ds((1 + i) * pitch + 7, 1), :] = stage[0, i : i + 1, :]
+        pext[pl.ds((1 + i) * pitch + 8 + span, 1), :] = stage[1, i : i + 1, :]
+    pext[pl.ds(halo_base + 7, 1), :] = recv_cor[0, 0:1, :].astype(jnp.float32)
+    pext[pl.ds(halo_base + 8 + span, 1), :] = recv_cor[1, 0:1, :].astype(jnp.float32)
 
     def shift_body(i, carry):
         window = pext[pl.ds(pl.multiple_of(i * pitch, 8), pitch), :]
@@ -220,11 +229,15 @@
             pltpu.VMEM((3, (row_count + 2) * col_count, wide), jnp.float32),
             pltpu.VMEM((9, col_count, wide), jnp.float32),
             pltpu.VMEM((col_count, wide), jnp.float32),
-            pltpu.VMEM((4, row_count, wide), jnp.float32),
-            pltpu.VMEM((4, row_count, wide), jnp.float32),
-            pltpu.VMEM((col_count, wide), jnp.float32),
+            pltpu.VMEM((2, row_count, wide), jnp.bfloat16),
+            pltpu.VMEM((2, row_count, wide), jnp.bfloat16),
+            pltpu.VMEM((col_count, wide), jnp.bfloat16),
             pltpu.VMEM((flat, width), jnp.bfloat16),
             pltpu.VMEM((flat, width), jnp.bfloat16),
+            pltpu.VMEM((2, row_count, wide), jnp.float32),
+            pltpu.VMEM((col_count, wide), jnp.bfloat16),
+            pltpu.VMEM((2, 16, wide), jnp.bfloat16),
+            pltpu.VMEM((2, 16, wide), jnp.bfloat16),
             pltpu.VMEM((2 * flat, width), jnp.float32),
             pltpu.VMEM((2 * row_count, 8, width), jnp.float32),
             pltpu.VMEM((flat, width), jnp.float32),

time: 26.1 us -> 23.5 us (0.900)
  Pallas kernels: 24 us -> 21.5 us
    pallas_call x1, Pallas kernels: 24 us -> 21.5 us  [on_device(): pl.pallas_call(functools.partial(layer_kernel, row_count, col_count, pitc...]
where the time goes in v8:
time: 23.5 us; the launch traced here: 23.4 us
  Pallas kernels  21.5 us (91%)
  local copies, waits for them, and re-layouts  1.87 us (8%)
    pallas_call x1, Pallas kernels, on_device(): pl.pallas_call(functools.partial(layer_kernel, row_count, col_count, pitc...  21.5 us
    unnamed x1, local copies, waits for them, and re-layouts  1.87 us

profile of v8, /device:TPU:161, one launch (start us, length us, event | category | flops | bytes accessed | tf_op | source)
XLA Modules:
  0.0 23.4 jit_solution(8602664686037762340)
XLA Ops:
  0.0 21.5 %shard_map.73 = bf16[1024,256]{1,0:T(8,128)(2,1)} custom-call(bf16[1024,256]{1,0:T(8,128)(2,1)} %bitcast.3, bf16[256,768]{1,0:T(8,128)(2,1)} %w_hbm.1, bf16[3,3,768]{2,1,0:T(4,128)(2,1)} %k_hbm.1, f32[768]{0:T(1024)} %b_hbm.1, bf16[64,256]{1,0:T(8,128)(2,1)} %filt_hbm.1, f32[256]{0:T(256)} %gain_hbm.1, bf16[256,256]{1,0:T(8,128)(2,1)} %wout_hbm.1), custom_call_target="tpu_custom_call" | custom-call | tf_op jit(solution)/shard_map/pallas_call | solution.py:214
  21.5 1.9 %copy.9 = bf16[32,32,256]{2,1,0:T(8,128)(2,1)} copy(bf16[32,32,256]{2,1,0:T(8,128)(2,1)} %bitcast.2) | data formatting | bytes 1048576

commit v9 on v8

--- a/solution.py
+++ b/solution.py
@@ -200,8 +200,18 @@
         return carry
 
     lax.fori_loop(0, (span // 8) * lane_groups, prev_pass, 0)
+    out_ref[...] = gated[...].astype(out_ref.dtype)
+
+
+def project_kernel(g_hbm, w_hbm, out_ref, g_ref, w_ref, sem):
+    loads = [pltpu.make_async_copy(g_hbm, g_ref, sem.at[0]),
+             pltpu.make_async_copy(w_hbm, w_ref, sem.at[1])]
+    for cp in loads:
+        cp.start()
+    for cp in loads:
+        cp.wait()
     out_ref[...] = jnp.dot(
-        gated[...].astype(jnp.bfloat16), wout_ref[...], preferred_element_type=jnp.float32
+        g_ref[...], w_ref[...], preferred_element_type=jnp.float32
     ).astype(out_ref.dtype)
 
 
@@ -257,6 +267,17 @@
         skip_gain,
         w_out,
     )
+    out = pl.pallas_call(
+        project_kernel,
+        out_shape=jax.ShapeDtypeStruct((flat, width), jnp.bfloat16),
+        in_specs=[pl.BlockSpec(memory_space=pl.ANY)] * 2,
+        out_specs=vmem,
+        scratch_shapes=[
+            pltpu.VMEM((flat, width), jnp.bfloat16),
+            pltpu.VMEM(w_out.shape, jnp.bfloat16),
+            pltpu.SemaphoreType.DMA((2,)),
+        ],
+    )(out, w_out)
     return out.reshape(row_count, col_count, width)
 
 

time: 23.5 us -> 23.4 us (level)
  local copies, waits for them, and re-layouts: 1.87 us -> 0 us
  Pallas kernels: 21.5 us -> 23.2 us
    pallas_call x0 -> x1, Pallas kernels: none -> 2.16 us  [on_device(): pl.pallas_call(project_kernel, out_shape=jax.ShapeDtypeStruct((flat, widt...]
    unnamed x1 -> x0, local copies, waits for them, and re-layouts: 1.87 us -> none
    pallas_call x1, Pallas kernels: 21.5 us -> 21 us  [on_device(): pl.pallas_call(functools.partial(layer_kernel, row_count, col_count, pitc...]
where the time goes in v9:
time: 23.4 us; the launch traced here: 23.2 us
  Pallas kernels  23.2 us (99%)
    pallas_call x1, Pallas kernels, on_device(): pl.pallas_call(functools.partial(layer_kernel, row_count, col_count, pitc...  21 us
    pallas_call x1, Pallas kernels, on_device(): pl.pallas_call(project_kernel, out_shape=jax.ShapeDtypeStruct((flat, widt...  2.16 us

profile of v9, /device:TPU:161, one launch (start us, length us, event | category | flops | bytes accessed | tf_op | source)
XLA Modules:
  0.0 23.2 jit_solution(17304445620476707525)
XLA Ops:
  0.0 21.0 %shard_map.73.g_hbm = bf16[1024,256]{1,0:T(8,128)(2,1)} custom-call(bf16[1024,256]{1,0:T(8,128)(2,1)} %bitcast.2, bf16[256,768]{1,0:T(8,128)(2,1)} %w_hbm.2, bf16[3,3,768]{2,1,0:T(4,128)(2,1)} %k_hbm.1, f32[768]{0:T(1024)} %b_hbm.1, bf16[64,256]{1,0:T(8,128)(2,1)} %filt_hbm.1, f32[256]{0:T(256)} %gain_hbm.1, bf16[256,256]{1,0:T(8,128)(2,1)} %w_hbm.3), custom_call_target="tpu_custom_call" | custom-call | tf_op jit(solution)/shard_map/pallas_call | solution.py:224
  21.0 2.2 %shard_map.74 = bf16[1024,256]{1,0:T(8,128)(2,1)} custom-call(bf16[1024,256]{1,0:T(8,128)(2,1)} %shard_map.73.g_hbm, bf16[256,256]{1,0:T(8,128)(2,1)} %w_hbm.3), custom_call_target="tpu_custom_call" | custom-call | tf_op jit(solution)/shard_map/pallas_call | solution.py:270

commit v10 on v9

--- a/solution.py
+++ b/solution.py
@@ -80,14 +80,9 @@
                                      device_id=peers[slot], device_id_type=mesh_id)
         for slot, (src_ref, dst_ref) in enumerate(pairs)
     ]
-    piece = 8 * span
-    pieces = rows // 8
-
-    def product_copy(k):
-        return pltpu.make_async_remote_copy(
-            own_b.at[pl.ds(k * piece, piece)], prev_b.at[pl.ds(k * piece, piece)],
-            send_sem.at[5 + k], recv_sem.at[5 + k], device_id=peers[5],
-            device_id_type=mesh_id)
+    product_copy = pltpu.make_async_remote_copy(
+        own_b, prev_b, send_sem.at[5], recv_sem.at[5], device_id=peers[5],
+        device_id_type=mesh_id)
     send_when = (c < ncol - 1, c > 0, c < ncol - 1, c > 0, None)
     recv_when = (c > 0, c < ncol - 1, c > 0, c < ncol - 1, None)
 
@@ -103,20 +98,10 @@
         cp.wait()
     for lag in range(2 * rows):
         fb[lag] = jnp.broadcast_to(filt_ref[lag : lag + 1, :].astype(jnp.float32), (8, width))
-    for cp, cond in zip(copies, send_when):
-        guarded(cond, cp.wait_send)
-    for cp, cond in zip(copies, recv_when):
-        guarded(cond, cp.wait_recv)
-
+    copies[4].wait_send()
+    copies[4].wait_recv()
     halo_base = pl.multiple_of(partner * (rows + 1) * pitch, 8)
     pext[pl.ds(halo_base + 8, span), :] = recv_row[...].astype(jnp.float32)
-    stage[0] = recv_col[0].astype(jnp.float32)
-    stage[1] = recv_col[1].astype(jnp.float32)
-    for i in range(rows):
-        pext[pl.ds((1 + i) * pitch + 7, 1), :] = stage[0, i : i + 1, :]
-        pext[pl.ds((1 + i) * pitch + 8 + span, 1), :] = stage[1, i : i + 1, :]
-    pext[pl.ds(halo_base + 7, 1), :] = recv_cor[0, 0:1, :].astype(jnp.float32)
-    pext[pl.ds(halo_base + 8 + span, 1), :] = recv_cor[1, 0:1, :].astype(jnp.float32)
 
     def shift_body(i, carry):
         window = pext[pl.ds(pl.multiple_of(i * pitch, 8), pitch), :]
@@ -126,36 +111,31 @@
         shifted[2, dst, :] = window[9 : 9 + span]
         return carry
 
-    lax.fori_loop(0, rows + 2, shift_body, 0)
-
-    def row_body(i, carry):
-        @pl.when(jnp.logical_and(r == 0, jnp.logical_and(i > 0, i % 8 == 0)))
-        def _():
-            product_copy(i // 8 - 1).start()
-
+    def depthwise(i, w0, size):
         res = []
         for grp in range(3):
             lanes = pl.ds(grp * width, width)
-            acc = bb[:, lanes]
+            acc = bb[0:size, lanes]
             for a in range(3):
-                src = pl.ds(pl.multiple_of((i + a) * span, 8), span)
+                src = pl.ds(pl.multiple_of((i + a) * span, 8) + w0, size)
                 for b in range(3):
-                    acc = acc + shifted[b, src, lanes] * kb[a * 3 + b, :, lanes]
+                    acc = acc + shifted[b, src, lanes] * kb[a * 3 + b, 0:size, lanes]
             res.append(acc.astype(jnp.bfloat16).astype(jnp.float32))
-        dst = pl.ds(pl.multiple_of(i * span, 16), span)
-        qf[dst, :] = res[0]
-        prod = (res[1] * res[2]).astype(jnp.bfloat16)
-        own_b[dst, :] = prod
-        ext[pl.ds(pl.multiple_of(count + i * span, 16), span), :] = prod.astype(jnp.float32)
-        return carry
-
-    lax.fori_loop(0, rows, row_body, 0)
-
-    @pl.when(r == 0)
-    def _():
-        product_copy(pieces - 1).start()
+        qf[pl.ds(pl.multiple_of(i * span, 8) + w0, size), :] = res[0]
+        ext[pl.ds(pl.multiple_of(count + i * span, 8) + w0, size), :] = (
+            (res[1] * res[2]).astype(jnp.bfloat16).astype(jnp.float32))
+
+    def inner_body(i, carry):
+        depthwise(i, 8, span - 16)
+        return carry
+
+    def outer_body(i, carry):
+        depthwise(i, 0, 8)
+        depthwise(i, span - 8, 8)
+        return carry
 
     lane_groups = width // 128
+    chunks = (span // 8) * lane_groups
 
     def own_pass(i, carry):
         lanes = pl.ds(pl.multiple_of((i % lane_groups) * 128, 128), 128)
@@ -170,18 +150,40 @@
             gated[pl.ds(a * span + w0, 8), lanes] = acc[a]
         return carry
 
-    lax.fori_loop(0, (span // 8) * lane_groups, own_pass, 0)
+    lax.fori_loop(0, rows + 2, shift_body, 0)
+    lax.fori_loop(0, rows, inner_body, 0)
+    lax.fori_loop(lane_groups, chunks - lane_groups, own_pass, 0)
+
+    for cp, cond in zip(copies[:4], send_when[:4]):
+        guarded(cond, cp.wait_send)
+    for cp, cond in zip(copies[:4], recv_when[:4]):
+        guarded(cond, cp.wait_recv)
+    stage[0] = recv_col[0].astype(jnp.float32)
+    stage[1] = recv_col[1].astype(jnp.float32)
+    for i in range(rows):
+        pext[pl.ds((1 + i) * pitch + 7, 1), :] = stage[0, i : i + 1, :]
+        pext[pl.ds((1 + i) * pitch + 8 + span, 1), :] = stage[1, i : i + 1, :]
+    pext[pl.ds(halo_base + 7, 1), :] = recv_cor[0, 0:1, :].astype(jnp.float32)
+    pext[pl.ds(halo_base + 8 + span, 1), :] = recv_cor[1, 0:1, :].astype(jnp.float32)
+    lax.fori_loop(0, rows + 2, shift_body, 0)
+    lax.fori_loop(0, rows, outer_body, 0)
+    own_b[...] = ext[count : 2 * count, :].astype(jnp.bfloat16)
 
     @pl.when(r == 0)
     def _():
-        for k in range(pieces):
-            product_copy(k).wait_send()
+        product_copy.start()
+
+    lax.fori_loop(0, lane_groups, own_pass, 0)
+    lax.fori_loop(chunks - lane_groups, chunks, own_pass, 0)
+
+    @pl.when(r == 0)
+    def _():
+        product_copy.wait_send()
         ext[0:count, :] = jnp.zeros((count, width), jnp.float32)
 
     @pl.when(r == 1)
     def _():
-        for k in range(pieces):
-            product_copy(k).wait_recv()
+        product_copy.wait_recv()
         ext[0:count, :] = prev_b[...].astype(jnp.float32)
 
     def prev_pass(i, carry):
@@ -252,8 +254,8 @@
             pltpu.VMEM((2 * row_count, 8, width), jnp.float32),
             pltpu.VMEM((flat, width), jnp.float32),
             pltpu.VMEM((flat, width), jnp.float32),
-            pltpu.SemaphoreType.DMA((5 + row_count // 8,)),
-            pltpu.SemaphoreType.DMA((5 + row_count // 8,)),
+            pltpu.SemaphoreType.DMA((6,)),
+            pltpu.SemaphoreType.DMA((6,)),
         ],
         compiler_params=pltpu.CompilerParams(
             collective_id=0, has_side_effects=True, vmem_limit_bytes=67043328

time: 23.4 us -> 21.6 us (0.923)
  Pallas kernels: 23.2 us -> 21.5 us
    pallas_call x1, Pallas kernels: 21 us -> 19.3 us  [on_device(): pl.pallas_call(functools.partial(layer_kernel, row_count, col_count, pitc...]
where the time goes in v10:
time: 21.6 us; the launch traced here: 21.5 us
  Pallas kernels  21.5 us (100%)
    pallas_call x1, Pallas kernels, on_device(): pl.pallas_call(functools.partial(layer_kernel, row_count, col_count, pitc...  19.3 us
    pallas_call x1, Pallas kernels, on_device(): pl.pallas_call(project_kernel, out_shape=jax.ShapeDtypeStruct((flat, widt...  2.17 us

profile of v10, /device:TPU:161, one launch (start us, length us, event | category | flops | bytes accessed | tf_op | source)
XLA Modules:
  0.0 21.5 jit_solution(10124345678550897372)
XLA Ops:
  0.0 19.3 %shard_map.73.g_hbm = bf16[1024,256]{1,0:T(8,128)(2,1)} custom-call(bf16[1024,256]{1,0:T(8,128)(2,1)} %bitcast.2, bf16[256,768]{1,0:T(8,128)(2,1)} %w_hbm.2, bf16[3,3,768]{2,1,0:T(4,128)(2,1)} %k_hbm.1, f32[768]{0:T(1024)} %b_hbm.1, bf16[64,256]{1,0:T(8,128)(2,1)} %filt_hbm.1, f32[256]{0:T(256)} %gain_hbm.1, bf16[256,256]{1,0:T(8,128)(2,1)} %w_hbm.3), custom_call_target="tpu_custom_call" | custom-call | tf_op jit(solution)/shard_map/pallas_call | solution.py:226
  19.3 2.2 %shard_map.74 = bf16[1024,256]{1,0:T(8,128)(2,1)} custom-call(bf16[1024,256]{1,0:T(8,128)(2,1)} %shard_map.73.g_hbm, bf16[256,256]{1,0:T(8,128)(2,1)} %w_hbm.3), custom_call_target="tpu_custom_call" | custom-call | tf_op jit(solution)/shard_map/pallas_call | solution.py:272

commit v11 on v10

--- a/solution.py
+++ b/solution.py
@@ -203,18 +203,6 @@
 
     lax.fori_loop(0, (span // 8) * lane_groups, prev_pass, 0)
     out_ref[...] = gated[...].astype(out_ref.dtype)
-
-
-def project_kernel(g_hbm, w_hbm, out_ref, g_ref, w_ref, sem):
-    loads = [pltpu.make_async_copy(g_hbm, g_ref, sem.at[0]),
-             pltpu.make_async_copy(w_hbm, w_ref, sem.at[1])]
-    for cp in loads:
-        cp.start()
-    for cp in loads:
-        cp.wait()
-    out_ref[...] = jnp.dot(
-        g_ref[...], w_ref[...], preferred_element_type=jnp.float32
-    ).astype(out_ref.dtype)
 
 
 def on_device(image_tokens, w_in, conv_kernel, conv_bias, long_filter, skip_gain, w_out):
@@ -269,17 +257,7 @@
         skip_gain,
         w_out,
     )
-    out = pl.pallas_call(
-        project_kernel,
-        out_shape=jax.ShapeDtypeStruct((flat, width), jnp.bfloat16),
-        in_specs=[pl.BlockSpec(memory_space=pl.ANY)] * 2,
-        out_specs=vmem,
-        scratch_shapes=[
-            pltpu.VMEM((flat, width), jnp.bfloat16),
-            pltpu.VMEM(w_out.shape, jnp.bfloat16),
-            pltpu.SemaphoreType.DMA((2,)),
-        ],
-    )(out, w_out)
+    out = jnp.dot(out, w_out, preferred_element_type=jnp.float32).astype(jnp.bfloat16)
     return out.reshape(row_count, col_count, width)
 
 

time: 21.6 us -> 21.6 us (level)
  Pallas kernels: 21.5 us -> 19.3 us
  matrix products: 0 us -> 2.16 us
    pallas_call x1 -> x0, Pallas kernels: 2.17 us -> none  [on_device(): pl.pallas_call(project_kernel, out_shape=jax.ShapeDtypeStruct((flat, widt...]
    dot_general x0 -> x1, matrix products: none -> 2.16 us  [on_device(): jnp.dot(out, w_out, preferred_element_type=jnp.float32).astype(jnp.bfloat16)]
where the time goes in v11:
time: 21.6 us; the launch traced here: 21.5 us
  Pallas kernels  19.3 us (89%)
  matrix products  2.16 us (10%)
    pallas_call x1, Pallas kernels, on_device(): pl.pallas_call(functools.partial(layer_kernel, row_count, col_count, pitc...  19.3 us
    dot_general x1, matrix products, on_device(): jnp.dot(out, w_out, preferred_element_type=jnp.float32).astype(jnp.bfloat16)  2.16 us

profile of v11, /device:TPU:161, one launch (start us, length us, event | category | flops | bytes accessed | tf_op | source)
XLA Modules:
  0.0 21.5 jit_solution(2075704282965921336)
XLA Ops:
  0.0 19.3 %shard_map.73 = bf16[1024,256]{1,0:T(8,128)(2,1)} custom-call(bf16[1024,256]{1,0:T(8,128)(2,1)} %bitcast.4, bf16[256,768]{1,0:T(8,128)(2,1)} %w_hbm.1, bf16[3,3,768]{2,1,0:T(4,128)(2,1)} %k_hbm.1, f32[768]{0:T(1024)} %b_hbm.1, bf16[64,256]{1,0:T(8,128)(2,1)} %filt_hbm.1, f32[256]{0:T(256)} %gain_hbm.1, bf16[256,256]{1,0:T(8,128)(2,1)} %wout_hbm.1), custom_call_target="tpu_custom_call" | custom-call | tf_op jit(solution)/shard_map/pallas_call | solution.py:214
  19.3 2.2 %convolution_convert_fusion = bf16[1024,256]{1,0:T(8,128)(2,1)} fusion(bf16[1024,256]{1,0:T(8,128)(2,1)} %shard_map.73, bf16[256,256]{1,0:T(8,128)(2,1)} %wout_hbm.1), kind=kOutput, calls=%fused_computation | convolution fusion | flops 134479872 | bytes 1179648 | tf_op jit(solution)/shard_map/dot_general | solution.py:260

commit v12 on v11

--- a/solution.py
+++ b/solution.py
@@ -10,7 +10,7 @@
 
 def layer_kernel(rows, span, pitch, x_hbm, w_hbm, k_hbm, b_hbm, filt_hbm, gain_hbm, wout_hbm,
                  out_ref, x_ref, w_ref, k_ref, b_ref, filt_ref, gain_ref, wout_ref, load_sem, pext,
-                 shifted, kb, bb, send_col, recv_col, recv_row, own_b, prev_b, stage, send_row,
+                 shifted, kb, bb, send_col, recv_col, recv_row, stage, send_row,
                  send_cor, recv_cor, ext, fb, qf, gated, send_sem, recv_sem):
     width = out_ref.shape[1]
     wide = w_ref.shape[1]
@@ -80,9 +80,14 @@
                                      device_id=peers[slot], device_id_type=mesh_id)
         for slot, (src_ref, dst_ref) in enumerate(pairs)
     ]
-    product_copy = pltpu.make_async_remote_copy(
-        own_b, prev_b, send_sem.at[5], recv_sem.at[5], device_id=peers[5],
-        device_id_type=mesh_id)
+    spans = ((8, span - 16), (0, 8), (span - 8, 8))
+    product_copies = [
+        pltpu.make_async_remote_copy(
+            ext.at[pl.ds(rows, rows), pl.ds(w0, size), :],
+            ext.at[pl.ds(0, rows), pl.ds(w0, size), :],
+            send_sem.at[5 + k], recv_sem.at[5 + k], device_id=peers[5], device_id_type=mesh_id)
+        for k, (w0, size) in enumerate(spans)
+    ]
     send_when = (c < ncol - 1, c > 0, c < ncol - 1, c > 0, None)
     recv_when = (c > 0, c < ncol - 1, c > 0, c < ncol - 1, None)
 
@@ -122,7 +127,7 @@
                     acc = acc + shifted[b, src, lanes] * kb[a * 3 + b, 0:size, lanes]
             res.append(acc.astype(jnp.bfloat16).astype(jnp.float32))
         qf[pl.ds(pl.multiple_of(i * span, 8) + w0, size), :] = res[0]
-        ext[pl.ds(pl.multiple_of(count + i * span, 8) + w0, size), :] = (
+        ext[rows + i, pl.ds(w0, size), :] = (
             (res[1] * res[2]).astype(jnp.bfloat16).astype(jnp.float32))
 
     def inner_body(i, carry):
@@ -142,7 +147,7 @@
         w0 = pl.multiple_of((i // lane_groups) * 8, 8)
         acc = [None] * rows
         for src in range(rows, 2 * rows):
-            x = ext[pl.ds(src * span + w0, 8), lanes]
+            x = ext[src, pl.ds(w0, 8), lanes]
             for a in range(src - rows, rows):
                 term = fb[rows + a - src, :, lanes] * x
                 acc[a] = term if acc[a] is None else acc[a] + term
@@ -150,9 +155,43 @@
             gated[pl.ds(a * span + w0, 8), lanes] = acc[a]
         return carry
 
+    def prev_pass(i, carry):
+        lanes = pl.ds(pl.multiple_of((i % lane_groups) * 128, 128), 128)
+        w0 = pl.multiple_of((i // lane_groups) * 8, 8)
+        acc = [gated[pl.ds(a * span + w0, 8), lanes] for a in range(rows)]
+        for src in range(rows):
+            x = ext[src, pl.ds(w0, 8), lanes]
+            for a in range(rows):
+                acc[a] = acc[a] + fb[rows + a - src, :, lanes] * x
+        gain = jnp.broadcast_to(gain_ref[lanes].reshape(1, 128), (8, 128))
+        for a in range(rows):
+            own = ext[rows + a, pl.ds(w0, 8), lanes]
+            q = qf[pl.ds(a * span + w0, 8), lanes]
+            gated[pl.ds(a * span + w0, 8), lanes] = q * (acc[a] + gain * own)
+        return carry
+
+    @pl.when(r == 0)
+    def _():
+        ext[0:rows] = jnp.zeros((rows, span, width), jnp.float32)
+
     lax.fori_loop(0, rows + 2, shift_body, 0)
     lax.fori_loop(0, rows, inner_body, 0)
+
+    @pl.when(r == 0)
+    def _():
+        product_copies[0].start()
+
     lax.fori_loop(lane_groups, chunks - lane_groups, own_pass, 0)
+
+    @pl.when(r == 1)
+    def _():
+        product_copies[0].wait_recv()
+
+    lax.fori_loop(lane_groups, chunks - lane_groups, prev_pass, 0)
+
+    @pl.when(r == 0)
+    def _():
+        product_copies[0].wait_send()
 
     for cp, cond in zip(copies[:4], send_when[:4]):
         guarded(cond, cp.wait_send)
@@ -167,41 +206,27 @@
     pext[pl.ds(halo_base + 8 + span, 1), :] = recv_cor[1, 0:1, :].astype(jnp.float32)
     lax.fori_loop(0, rows + 2, shift_body, 0)
     lax.fori_loop(0, rows, outer_body, 0)
-    own_b[...] = ext[count : 2 * count, :].astype(jnp.bfloat16)
-
-    @pl.when(r == 0)
-    def _():
-        product_copy.start()
+
+    @pl.when(r == 0)
+    def _():
+        product_copies[1].start()
+        product_copies[2].start()
 
     lax.fori_loop(0, lane_groups, own_pass, 0)
     lax.fori_loop(chunks - lane_groups, chunks, own_pass, 0)
 
-    @pl.when(r == 0)
-    def _():
-        product_copy.wait_send()
-        ext[0:count, :] = jnp.zeros((count, width), jnp.float32)
-
     @pl.when(r == 1)
     def _():
-        product_copy.wait_recv()
-        ext[0:count, :] = prev_b[...].astype(jnp.float32)
-
-    def prev_pass(i, carry):
-        lanes = pl.ds(pl.multiple_of((i % lane_groups) * 128, 128), 128)
-        w0 = pl.multiple_of((i // lane_groups) * 8, 8)
-        acc = [gated[pl.ds(a * span + w0, 8), lanes] for a in range(rows)]
-        for src in range(rows):
-            x = ext[pl.ds(src * span + w0, 8), lanes]
-            for a in range(rows):
-                acc[a] = acc[a] + fb[rows + a - src, :, lanes] * x
-        gain = jnp.broadcast_to(gain_ref[lanes].reshape(1, 128), (8, 128))
-        for a in range(rows):
-            own = ext[pl.ds(count + a * span + w0, 8), lanes]
-            q = qf[pl.ds(a * span + w0, 8), lanes]
-            gated[pl.ds(a * span + w0, 8), lanes] = q * (acc[a] + gain * own)
-        return carry
-
-    lax.fori_loop(0, (span // 8) * lane_groups, prev_pass, 0)
+        product_copies[1].wait_recv()
+        product_copies[2].wait_recv()
+
+    lax.fori_loop(0, lane_groups, prev_pass, 0)
+    lax.fori_loop(chunks - lane_groups, chunks, prev_pass, 0)
+
+    @pl.when(r == 0)
+    def _():
+        for cp in product_copies[1:]:
+            cp.wait_send()
     out_ref[...] = gated[...].astype(out_ref.dtype)
 
 
@@ -232,18 +257,16 @@
             pltpu.VMEM((2, row_count, wide), jnp.bfloat16),
             pltpu.VMEM((2, row_count, wide), jnp.bfloat16),
             pltpu.VMEM((col_count, wide), jnp.bfloat16),
-            pltpu.VMEM((flat, width), jnp.bfloat16),
-            pltpu.VMEM((flat, width), jnp.bfloat16),
             pltpu.VMEM((2, row_count, wide), jnp.float32),
             pltpu.VMEM((col_count, wide), jnp.bfloat16),
             pltpu.VMEM((2, 16, wide), jnp.bfloat16),
             pltpu.VMEM((2, 16, wide), jnp.bfloat16),
-            pltpu.VMEM((2 * flat, width), jnp.float32),
+            pltpu.VMEM((2 * row_count, col_count, width), jnp.float32),
             pltpu.VMEM((2 * row_count, 8, width), jnp.float32),
             pltpu.VMEM((flat, width), jnp.float32),
             pltpu.VMEM((flat, width), jnp.float32),
-            pltpu.SemaphoreType.DMA((6,)),
-            pltpu.SemaphoreType.DMA((6,)),
+            pltpu.SemaphoreType.DMA((8,)),
+            pltpu.SemaphoreType.DMA((8,)),
         ],
         compiler_params=pltpu.CompilerParams(
             collective_id=0, has_side_effects=True, vmem_limit_bytes=67043328

time: 21.6 us -> 21.4 us (level)
  no operation moved by 1% of the time
where the time goes in v12:
time: 21.4 us; the launch traced here: 21.3 us
  Pallas kernels  19.1 us (89%)
  matrix products  2.15 us (10%)
    pallas_call x1, Pallas kernels, on_device(): pl.pallas_call(functools.partial(layer_kernel, row_count, col_count, pitc...  19.1 us
    dot_general x1, matrix products, on_device(): jnp.dot(out, w_out, preferred_element_type=jnp.float32).astype(jnp.bfloat16)  2.15 us

profile of v12, /device:TPU:161, one launch (start us, length us, event | category | flops | bytes accessed | tf_op | source)
XLA Modules:
  0.0 21.3 jit_solution(16947289500671291995)
XLA Ops:
  0.0 19.1 %shard_map.73 = bf16[1024,256]{1,0:T(8,128)(2,1)} custom-call(bf16[1024,256]{1,0:T(8,128)(2,1)} %bitcast.4, bf16[256,768]{1,0:T(8,128)(2,1)} %w_hbm.1, bf16[3,3,768]{2,1,0:T(4,128)(2,1)} %k_hbm.1, f32[768]{0:T(1024)} %b_hbm.1, bf16[64,256]{1,0:T(8,128)(2,1)} %filt_hbm.1, f32[256]{0:T(256)} %gain_hbm.1, bf16[256,256]{1,0:T(8,128)(2,1)} %wout_hbm.1), custom_call_target="tpu_custom_call" | custom-call | tf_op jit(solution)/shard_map/pallas_call | solution.py:239
  19.1 2.2 %convolution_convert_fusion = bf16[1024,256]{1,0:T(8,128)(2,1)} fusion(bf16[1024,256]{1,0:T(8,128)(2,1)} %shard_map.73, bf16[256,256]{1,0:T(8,128)(2,1)} %wout_hbm.1), kind=kOutput, calls=%fused_computation | convolution fusion | flops 134479872 | bytes 1179648 | tf_op jit(solution)/shard_map/dot_general | solution.py:283

commit v13 on v12

--- a/solution.py
+++ b/solution.py
@@ -71,6 +71,35 @@
     send_cor[1] = jnp.broadcast_to(pext[pl.ds(edge_base + 8, 1), :],
                                    (corner_rows, wide)).astype(jnp.bfloat16)
 
+    def shift_body(i, carry):
+        window = pext[pl.ds(pl.multiple_of(i * pitch, 8), pitch), :]
+        dst = pl.ds(pl.multiple_of(i * span, 8), span)
+        shifted[0, dst, :] = window[7 : 7 + span]
+        shifted[1, dst, :] = window[8 : 8 + span]
+        shifted[2, dst, :] = window[9 : 9 + span]
+        return carry
+
+    def depthwise(i, w0, size):
+        res = []
+        for grp in range(3):
+            lanes = pl.ds(grp * width, width)
+            acc = bb[0:size, lanes]
+            for a in range(3):
+                src = pl.ds(pl.multiple_of((i + a) * span, 8) + w0, size)
+                for b in range(3):
+                    acc = acc + shifted[b, src, lanes] * kb[a * 3 + b, 0:size, lanes]
+            res.append(acc.astype(jnp.bfloat16).astype(jnp.float32))
+        qf[pl.ds(pl.multiple_of(i * span, 8) + w0, size), :] = res[0]
+        ext[rows + i, pl.ds(w0, size), :] = (
+            (res[1] * res[2]).astype(jnp.bfloat16).astype(jnp.float32))
+
+    def inner_body(i, carry):
+        depthwise(i, 8, span - 16)
+        return carry
+
+    lax.fori_loop(0, rows + 2, shift_body, 0)
+    lax.fori_loop(r, r + rows - 1, inner_body, 0)
+
     pl.semaphore_wait(barrier, 1 + 2 * has_left + 2 * has_right)
     pairs = ((send_col.at[0], recv_col.at[0]), (send_col.at[1], recv_col.at[1]),
              (send_cor.at[0], recv_cor.at[0]), (send_cor.at[1], recv_cor.at[1]),
@@ -108,32 +137,6 @@
     halo_base = pl.multiple_of(partner * (rows + 1) * pitch, 8)
     pext[pl.ds(halo_base + 8, span), :] = recv_row[...].astype(jnp.float32)
 
-    def shift_body(i, carry):
-        window = pext[pl.ds(pl.multiple_of(i * pitch, 8), pitch), :]
-        dst = pl.ds(pl.multiple_of(i * span, 8), span)
-        shifted[0, dst, :] = window[7 : 7 + span]
-        shifted[1, dst, :] = window[8 : 8 + span]
-        shifted[2, dst, :] = window[9 : 9 + span]
-        return carry
-
-    def depthwise(i, w0, size):
-        res = []
-        for grp in range(3):
-            lanes = pl.ds(grp * width, width)
-            acc = bb[0:size, lanes]
-            for a in range(3):
-                src = pl.ds(pl.multiple_of((i + a) * span, 8) + w0, size)
-                for b in range(3):
-                    acc = acc + shifted[b, src, lanes] * kb[a * 3 + b, 0:size, lanes]
-            res.append(acc.astype(jnp.bfloat16).astype(jnp.float32))
-        qf[pl.ds(pl.multiple_of(i * span, 8) + w0, size), :] = res[0]
-        ext[rows + i, pl.ds(w0, size), :] = (
-            (res[1] * res[2]).astype(jnp.bfloat16).astype(jnp.float32))
-
-    def inner_body(i, carry):
-        depthwise(i, 8, span - 16)
-        return carry
-
     def outer_body(i, carry):
         depthwise(i, 0, 8)
         depthwise(i, span - 8, 8)
@@ -174,8 +177,8 @@
     def _():
         ext[0:rows] = jnp.zeros((rows, span, width), jnp.float32)
 
-    lax.fori_loop(0, rows + 2, shift_body, 0)
-    lax.fori_loop(0, rows, inner_body, 0)
+    shift_body(partner * (rows + 1), 0)
+    inner_body(partner * (rows - 1), 0)
 
     @pl.when(r == 0)
     def _():

time: 21.4 us -> 22.1 us (1.033)
  Pallas kernels: 19.1 us -> 19.8 us
    pallas_call x1, Pallas kernels: 19.1 us -> 19.8 us  [on_device(): pl.pallas_call(functools.partial(layer_kernel, row_count, col_count, pitc...]
where the time goes in v13:
time: 22.1 us; the launch traced here: 22 us
  Pallas kernels  19.8 us (90%)
  matrix products  2.15 us (10%)
    pallas_call x1, Pallas kernels, on_device(): pl.pallas_call(functools.partial(layer_kernel, row_count, col_count, pitc...  19.8 us
    dot_general x1, matrix products, on_device(): jnp.dot(out, w_out, preferred_element_type=jnp.float32).astype(jnp.bfloat16)  2.15 us

profile of v13, /device:TPU:161, one launch (start us, length us, event | category | flops | bytes accessed | tf_op | source)
XLA Modules:
  0.0 22.0 jit_solution(16603061150956552145)
XLA Ops:
  0.0 19.8 %shard_map.73 = bf16[1024,256]{1,0:T(8,128)(2,1)} custom-call(bf16[1024,256]{1,0:T(8,128)(2,1)} %bitcast.4, bf16[256,768]{1,0:T(8,128)(2,1)} %w_hbm.1, bf16[3,3,768]{2,1,0:T(4,128)(2,1)} %k_hbm.1, f32[768]{0:T(1024)} %b_hbm.1, bf16[64,256]{1,0:T(8,128)(2,1)} %filt_hbm.1, f32[256]{0:T(256)} %gain_hbm.1, bf16[256,256]{1,0:T(8,128)(2,1)} %wout_hbm.1), custom_call_target="tpu_custom_call" | custom-call | tf_op jit(solution)/shard_map/pallas_call | solution.py:242
  19.9 2.2 %convolution_convert_fusion = bf16[1024,256]{1,0:T(8,128)(2,1)} fusion(bf16[1024,256]{1,0:T(8,128)(2,1)} %shard_map.73, bf16[256,256]{1,0:T(8,128)(2,1)} %wout_hbm.1), kind=kOutput, calls=%fused_computation | convolution fusion | flops 134479872 | bytes 1179648 | tf_op jit(solution)/shard_map/dot_general | solution.py:286

commit v14 on v12

--- a/solution.py
+++ b/solution.py
@@ -80,14 +80,21 @@
                                      device_id=peers[slot], device_id_type=mesh_id)
         for slot, (src_ref, dst_ref) in enumerate(pairs)
     ]
-    spans = ((8, span - 16), (0, 8), (span - 8, 8))
     product_copies = [
         pltpu.make_async_remote_copy(
-            ext.at[pl.ds(rows, rows), pl.ds(w0, size), :],
-            ext.at[pl.ds(0, rows), pl.ds(w0, size), :],
-            send_sem.at[5 + k], recv_sem.at[5 + k], device_id=peers[5], device_id_type=mesh_id)
-        for k, (w0, size) in enumerate(spans)
+            ext.at[pl.ds(rows, rows), pl.ds(8, span - 16), :],
+            ext.at[pl.ds(0, rows), pl.ds(8, span - 16), :],
+            send_sem.at[5], recv_sem.at[5], device_id=peers[5], device_id_type=mesh_id)
     ]
+    pieces = rows // 8
+
+    def edge_copy(k, side):
+        w0 = side * (span - 8)
+        slot = 6 + 2 * k + side
+        return pltpu.make_async_remote_copy(
+            ext.at[pl.ds(rows + 8 * k, 8), pl.ds(w0, 8), :],
+            ext.at[pl.ds(8 * k, 8), pl.ds(w0, 8), :],
+            send_sem.at[slot], recv_sem.at[slot], device_id=peers[5], device_id_type=mesh_id)
     send_when = (c < ncol - 1, c > 0, c < ncol - 1, c > 0, None)
     recv_when = (c > 0, c < ncol - 1, c > 0, c < ncol - 1, None)
 
@@ -135,6 +142,11 @@
         return carry
 
     def outer_body(i, carry):
+        @pl.when(jnp.logical_and(r == 0, jnp.logical_and(i > 0, i % 8 == 0)))
+        def _():
+            edge_copy(i // 8 - 1, 0).start()
+            edge_copy(i // 8 - 1, 1).start()
+
         depthwise(i, 0, 8)
         depthwise(i, span - 8, 8)
         return carry
@@ -209,24 +221,26 @@
 
     @pl.when(r == 0)
     def _():
-        product_copies[1].start()
-        product_copies[2].start()
+        edge_copy(pieces - 1, 0).start()
+        edge_copy(pieces - 1, 1).start()
 
     lax.fori_loop(0, lane_groups, own_pass, 0)
     lax.fori_loop(chunks - lane_groups, chunks, own_pass, 0)
 
     @pl.when(r == 1)
     def _():
-        product_copies[1].wait_recv()
-        product_copies[2].wait_recv()
+        for k in range(pieces):
+            edge_copy(k, 0).wait_recv()
+            edge_copy(k, 1).wait_recv()
 
     lax.fori_loop(0, lane_groups, prev_pass, 0)
     lax.fori_loop(chunks - lane_groups, chunks, prev_pass, 0)
 
     @pl.when(r == 0)
     def _():
-        for cp in product_copies[1:]:
-            cp.wait_send()
+        for k in range(pieces):
+            edge_copy(k, 0).wait_send()
+            edge_copy(k, 1).wait_send()
     out_ref[...] = gated[...].astype(out_ref.dtype)
 
 
@@ -265,8 +279,8 @@
             pltpu.VMEM((2 * row_count, 8, width), jnp.float32),
             pltpu.VMEM((flat, width), jnp.float32),
             pltpu.VMEM((flat, width), jnp.float32),
-            pltpu.SemaphoreType.DMA((8,)),
-            pltpu.SemaphoreType.DMA((8,)),
+            pltpu.SemaphoreType.DMA((6 + 2 * (row_count // 8),)),
+            pltpu.SemaphoreType.DMA((6 + 2 * (row_count // 8),)),
         ],
         compiler_params=pltpu.CompilerParams(
             collective_id=0, has_side_effects=True, vmem_limit_bytes=67043328

time: 21.4 us -> 22.2 us (1.037)
  Pallas kernels: 19.1 us -> 19.9 us
    pallas_call x1, Pallas kernels: 19.1 us -> 19.9 us  [on_device(): pl.pallas_call(functools.partial(layer_kernel, row_count, col_count, pitc...]
where the time goes in v14:
time: 22.2 us; the launch traced here: 22.1 us
  Pallas kernels  19.9 us (90%)
  matrix products  2.15 us (10%)
    pallas_call x1, Pallas kernels, on_device(): pl.pallas_call(functools.partial(layer_kernel, row_count, col_count, pitc...  19.9 us
    dot_general x1, matrix products, on_device(): jnp.dot(out, w_out, preferred_element_type=jnp.float32).astype(jnp.bfloat16)  2.15 us

profile of v14, /device:TPU:161, one launch (start us, length us, event | category | flops | bytes accessed | tf_op | source)
XLA Modules:
  0.0 22.1 jit_solution(11203864566409987208)
XLA Ops:
  0.0 19.9 %shard_map.73 = bf16[1024,256]{1,0:T(8,128)(2,1)} custom-call(bf16[1024,256]{1,0:T(8,128)(2,1)} %bitcast.4, bf16[256,768]{1,0:T(8,128)(2,1)} %w_hbm.1, bf16[3,3,768]{2,1,0:T(4,128)(2,1)} %k_hbm.1, f32[768]{0:T(1024)} %b_hbm.1, bf16[64,256]{1,0:T(8,128)(2,1)} %filt_hbm.1, f32[256]{0:T(256)} %gain_hbm.1, bf16[256,256]{1,0:T(8,128)(2,1)} %wout_hbm.1), custom_call_target="tpu_custom_call" | custom-call | tf_op jit(solution)/shard_map/pallas_call | solution.py:253
  19.9 2.2 %convolution_convert_fusion = bf16[1024,256]{1,0:T(8,128)(2,1)} fusion(bf16[1024,256]{1,0:T(8,128)(2,1)} %shard_map.73, bf16[256,256]{1,0:T(8,128)(2,1)} %wout_hbm.1), kind=kOutput, calls=%fused_computation | convolution fusion | flops 134479872 | bytes 1179648 | tf_op jit(solution)/shard_map/dot_general | solution.py:297

commit v15 on v14

--- a/solution.py
+++ b/solution.py
@@ -80,17 +80,18 @@
                                      device_id=peers[slot], device_id_type=mesh_id)
         for slot, (src_ref, dst_ref) in enumerate(pairs)
     ]
-    product_copies = [
-        pltpu.make_async_remote_copy(
-            ext.at[pl.ds(rows, rows), pl.ds(8, span - 16), :],
-            ext.at[pl.ds(0, rows), pl.ds(8, span - 16), :],
-            send_sem.at[5], recv_sem.at[5], device_id=peers[5], device_id_type=mesh_id)
-    ]
     pieces = rows // 8
+
+    def inner_copy(k):
+        return pltpu.make_async_remote_copy(
+            ext.at[pl.ds(rows + 8 * k, 8), pl.ds(8, span - 16), :],
+            ext.at[pl.ds(8 * k, 8), pl.ds(8, span - 16), :],
+            send_sem.at[5 + 3 * k], recv_sem.at[5 + 3 * k], device_id=peers[5],
+            device_id_type=mesh_id)
 
     def edge_copy(k, side):
         w0 = side * (span - 8)
-        slot = 6 + 2 * k + side
+        slot = 6 + 3 * k + side
         return pltpu.make_async_remote_copy(
             ext.at[pl.ds(rows + 8 * k, 8), pl.ds(w0, 8), :],
             ext.at[pl.ds(8 * k, 8), pl.ds(w0, 8), :],
@@ -138,6 +139,10 @@
             (res[1] * res[2]).astype(jnp.bfloat16).astype(jnp.float32))
 
     def inner_body(i, carry):
+        @pl.when(jnp.logical_and(r == 0, jnp.logical_and(i > 0, i % 8 == 0)))
+        def _():
+            inner_copy(i // 8 - 1).start()
+
         depthwise(i, 8, span - 16)
         return carry
 
@@ -191,19 +196,21 @@
 
     @pl.when(r == 0)
     def _():
-        product_copies[0].start()
+        inner_copy(pieces - 1).start()
 
     lax.fori_loop(lane_groups, chunks - lane_groups, own_pass, 0)
 
     @pl.when(r == 1)
     def _():
-        product_copies[0].wait_recv()
+        for k in range(pieces):
+            inner_copy(k).wait_recv()
 
     lax.fori_loop(lane_groups, chunks - lane_groups, prev_pass, 0)
 
     @pl.when(r == 0)
     def _():
-        product_copies[0].wait_send()
+        for k in range(pieces):
+            inner_copy(k).wait_send()
 
     for cp, cond in zip(copies[:4], send_when[:4]):
         guarded(cond, cp.wait_send)
@@ -279,8 +286,8 @@
             pltpu.VMEM((2 * row_count, 8, width), jnp.float32),
             pltpu.VMEM((flat, width), jnp.float32),
             pltpu.VMEM((flat, width), jnp.float32),
-            pltpu.SemaphoreType.DMA((6 + 2 * (row_count // 8),)),
-            pltpu.SemaphoreType.DMA((6 + 2 * (row_count // 8),)),
+            pltpu.SemaphoreType.DMA((5 + 3 * (row_count // 8),)),
+            pltpu.SemaphoreType.DMA((5 + 3 * (row_count // 8),)),
         ],
         compiler_params=pltpu.CompilerParams(
             collective_id=0, has_side_effects=True, vmem_limit_bytes=67043328

time: 22.2 us -> 22.2 us (level)
  no operation moved by 1% of the time
where the time goes in v15:
time: 22.2 us; the launch traced here: 22.1 us
  Pallas kernels  19.9 us (90%)
  matrix products  2.16 us (10%)
    pallas_call x1, Pallas kernels, on_device(): pl.pallas_call(functools.partial(layer_kernel, row_count, col_count, pitc...  19.9 us
    dot_general x1, matrix products, on_device(): jnp.dot(out, w_out, preferred_element_type=jnp.float32).astype(jnp.bfloat16)  2.16 us

profile of v15, /device:TPU:161, one launch (start us, length us, event | category | flops | bytes accessed | tf_op | source)
XLA Modules:
  0.0 22.1 jit_solution(5279451971909306002)
XLA Ops:
  0.0 19.9 %shard_map.73 = bf16[1024,256]{1,0:T(8,128)(2,1)} custom-call(bf16[1024,256]{1,0:T(8,128)(2,1)} %bitcast.4, bf16[256,768]{1,0:T(8,128)(2,1)} %w_hbm.1, bf16[3,3,768]{2,1,0:T(4,128)(2,1)} %k_hbm.1, f32[768]{0:T(1024)} %b_hbm.1, bf16[64,256]{1,0:T(8,128)(2,1)} %filt_hbm.1, f32[256]{0:T(256)} %gain_hbm.1, bf16[256,256]{1,0:T(8,128)(2,1)} %wout_hbm.1), custom_call_target="tpu_custom_call" | custom-call | tf_op jit(solution)/shard_map/pallas_call | solution.py:260
  20.0 2.2 %convolution_convert_fusion = bf16[1024,256]{1,0:T(8,128)(2,1)} fusion(bf16[1024,256]{1,0:T(8,128)(2,1)} %shard_map.73, bf16[256,256]{1,0:T(8,128)(2,1)} %wout_hbm.1), kind=kOutput, calls=%fused_computation | convolution fusion | flops 134479872 | bytes 1179648 | tf_op jit(solution)/shard_map/dot_general | solution.py:304

commit v16 on v12

--- a/solution.py
+++ b/solution.py
@@ -227,7 +227,8 @@
     def _():
         for cp in product_copies[1:]:
             cp.wait_send()
-    out_ref[...] = gated[...].astype(out_ref.dtype)
+    out_ref[...] = jnp.dot(
+        gated[...].astype(jnp.bfloat16), wout_ref[...], preferred_element_type=jnp.float32)
 
 
 def on_device(image_tokens, w_in, conv_kernel, conv_bias, long_filter, skip_gain, w_out):
@@ -238,7 +239,7 @@
     vmem = pl.BlockSpec(memory_space=pltpu.VMEM)
     out = pl.pallas_call(
         functools.partial(layer_kernel, row_count, col_count, pitch),
-        out_shape=jax.ShapeDtypeStruct((flat, width), jnp.bfloat16),
+        out_shape=jax.ShapeDtypeStruct((flat, width), jnp.float32),
         in_specs=[pl.BlockSpec(memory_space=pl.ANY)] * 7,
         out_specs=vmem,
         scratch_shapes=[
@@ -280,7 +281,7 @@
         skip_gain,
         w_out,
     )
-    out = jnp.dot(out, w_out, preferred_element_type=jnp.float32).astype(jnp.bfloat16)
+    out = out.astype(jnp.bfloat16)
     return out.reshape(row_count, col_count, width)
 
 

time: 21.4 us -> 21.9 us (1.023)
  matrix products: 2.15 us -> 0 us
  other arithmetic: 0 us -> 2.07 us
  Pallas kernels: 19.1 us -> 19.7 us
    dot_general x1 -> x0, matrix products: 2.15 us -> none  [on_device(): jnp.dot(out, w_out, preferred_element_type=jnp.float32).astype(jnp.bfloat16)]
    convert_element_type x0 -> x1, other arithmetic: none -> 2.07 us  [on_device(): out = out.astype(jnp.bfloat16)]
    pallas_call x1, Pallas kernels: 19.1 us -> 19.7 us  [on_device(): pl.pallas_call(functools.partial(layer_kernel, row_count, col_count, pitc...]
where the time goes in v16:
time: 21.9 us; the launch traced here: 21.8 us
  Pallas kernels  19.7 us (90%)
  other arithmetic  2.07 us (9%)
    pallas_call x1, Pallas kernels, on_device(): pl.pallas_call(functools.partial(layer_kernel, row_count, col_count, pitc...  19.7 us
    convert_element_type x1, other arithmetic, on_device(): out = out.astype(jnp.bfloat16)  2.07 us

profile of v16, /device:TPU:161, one launch (start us, length us, event | category | flops | bytes accessed | tf_op | source)
XLA Modules:
  0.0 21.8 jit_solution(11691454355238829777)
XLA Ops:
  0.0 19.7 %shard_map.73 = f32[1024,256]{1,0:T(8,128)} custom-call(bf16[1024,256]{1,0:T(8,128)(2,1)} %bitcast.2, bf16[256,768]{1,0:T(8,128)(2,1)} %w_hbm.1, bf16[3,3,768]{2,1,0:T(4,128)(2,1)} %k_hbm.1, f32[768]{0:T(1024)} %b_hbm.1, bf16[64,256]{1,0:T(8,128)(2,1)} %filt_hbm.1, f32[256]{0:T(256)} %gain_hbm.1, bf16[256,256]{1,0:T(8,128)(2,1)} %wout_hbm.1), custom_call_target="tpu_custom_call" | custom-call | tf_op jit(solution)/shard_map/pallas_call | solution.py:240
  19.7 2.1 %convert_element_type.3 = bf16[1024,256]{1,0:T(8,128)(2,1)} convert(f32[1024,256]{1,0:T(8,128)} %shard_map.73) | non-fusion elementwise | flops 262144 | bytes 1572864 | tf_op jit(solution)/shard_map/convert_element_type | solution.py:284

commit v17 on v12

--- a/solution.py
+++ b/solution.py
@@ -47,10 +47,6 @@
         cp.start()
     for cp in loads[:4]:
         cp.wait()
-    for i in range(9):
-        kb[i] = jnp.broadcast_to(
-            k_ref[i // 3, i % 3 : i % 3 + 1, :].astype(jnp.float32), (span, wide))
-    bb[...] = jnp.broadcast_to(b_ref[...].reshape(1, wide), (span, wide))
     proj = jnp.dot(x_ref[...], w_ref[...], preferred_element_type=jnp.float32)
     proj = proj.astype(jnp.bfloat16).astype(jnp.float32)
     for i in range(rows):
@@ -99,6 +95,10 @@
 
     for cp, cond in zip(copies, send_when):
         guarded(cond, cp.start)
+    for i in range(9):
+        kb[i] = jnp.broadcast_to(
+            k_ref[i // 3, i % 3 : i % 3 + 1, :].astype(jnp.float32), (span, wide))
+    bb[...] = jnp.broadcast_to(b_ref[...].reshape(1, wide), (span, wide))
     for cp in loads[4:]:
         cp.wait()
     for lag in range(2 * rows):

time: 21.4 us -> 21.4 us (level)
  no operation moved by 1% of the time
where the time goes in v17:
time: 21.4 us; the launch traced here: 21.3 us
  Pallas kernels  19.1 us (89%)
  matrix products  2.15 us (10%)
    pallas_call x1, Pallas kernels, on_device(): pl.pallas_call(functools.partial(layer_kernel, row_count, col_count, pitc...  19.1 us
    dot_general x1, matrix products, on_device(): jnp.dot(out, w_out, preferred_element_type=jnp.float32).astype(jnp.bfloat16)  2.15 us

profile of v17, /device:TPU:161, one launch (start us, length us, event | category | flops | bytes accessed | tf_op | source)
XLA Modules:
  0.0 21.3 jit_solution(15159889164260135795)
XLA Ops:
  0.0 19.1 %shard_map.73 = bf16[1024,256]{1,0:T(8,128)(2,1)} custom-call(bf16[1024,256]{1,0:T(8,128)(2,1)} %bitcast.4, bf16[256,768]{1,0:T(8,128)(2,1)} %w_hbm.1, bf16[3,3,768]{2,1,0:T(4,128)(2,1)} %k_hbm.1, f32[768]{0:T(1024)} %b_hbm.1, bf16[64,256]{1,0:T(8,128)(2,1)} %filt_hbm.1, f32[256]{0:T(256)} %gain_hbm.1, bf16[256,256]{1,0:T(8,128)(2,1)} %wout_hbm.1), custom_call_target="tpu_custom_call" | custom-call | tf_op jit(solution)/shard_map/pallas_call | solution.py:239
  19.1 2.2 %convolution_convert_fusion = bf16[1024,256]{1,0:T(8,128)(2,1)} fusion(bf16[1024,256]{1,0:T(8,128)(2,1)} %shard_map.73, bf16[256,256]{1,0:T(8,128)(2,1)} %wout_hbm.1), kind=kOutput, calls=%fused_computation | convolution fusion | flops 134479872 | bytes 1179648 | tf_op jit(solution)/shard_map/dot_general | solution.py:283

commit v18 on v17

--- a/solution.py
+++ b/solution.py
@@ -200,11 +200,11 @@
     stage[0] = recv_col[0].astype(jnp.float32)
     stage[1] = recv_col[1].astype(jnp.float32)
     for i in range(rows):
-        pext[pl.ds((1 + i) * pitch + 7, 1), :] = stage[0, i : i + 1, :]
-        pext[pl.ds((1 + i) * pitch + 8 + span, 1), :] = stage[1, i : i + 1, :]
-    pext[pl.ds(halo_base + 7, 1), :] = recv_cor[0, 0:1, :].astype(jnp.float32)
-    pext[pl.ds(halo_base + 8 + span, 1), :] = recv_cor[1, 0:1, :].astype(jnp.float32)
-    lax.fori_loop(0, rows + 2, shift_body, 0)
+        shifted[0, pl.ds((1 + i) * span, 1), :] = stage[0, i : i + 1, :]
+        shifted[2, pl.ds((1 + i) * span + span - 1, 1), :] = stage[1, i : i + 1, :]
+    halo_at = pl.multiple_of(partner * (rows + 1) * span, 8)
+    shifted[0, pl.ds(halo_at, 1), :] = recv_cor[0, 0:1, :].astype(jnp.float32)
+    shifted[2, pl.ds(halo_at + span - 1, 1), :] = recv_cor[1, 0:1, :].astype(jnp.float32)
     lax.fori_loop(0, rows, outer_body, 0)
 
     @pl.when(r == 0)

time: 21.4 us -> 20.6 us (0.963)
  Pallas kernels: 19.1 us -> 18.3 us
    pallas_call x1, Pallas kernels: 19.1 us -> 18.3 us  [on_device(): pl.pallas_call(functools.partial(layer_kernel, row_count, col_count, pitc...]
where the time goes in v18:
time: 20.6 us; the launch traced here: 20.5 us
  Pallas kernels  18.3 us (89%)
  matrix products  2.16 us (10%)
    pallas_call x1, Pallas kernels, on_device(): pl.pallas_call(functools.partial(layer_kernel, row_count, col_count, pitc...  18.3 us
    dot_general x1, matrix products, on_device(): jnp.dot(out, w_out, preferred_element_type=jnp.float32).astype(jnp.bfloat16)  2.16 us

profile of v18, /device:TPU:161, one launch (start us, length us, event | category | flops | bytes accessed | tf_op | source)
XLA Modules:
  0.0 20.5 jit_solution(16240452750490323074)
XLA Ops:
  0.0 18.3 %shard_map.73 = bf16[1024,256]{1,0:T(8,128)(2,1)} custom-call(bf16[1024,256]{1,0:T(8,128)(2,1)} %bitcast.4, bf16[256,768]{1,0:T(8,128)(2,1)} %w_hbm.1, bf16[3,3,768]{2,1,0:T(4,128)(2,1)} %k_hbm.1, f32[768]{0:T(1024)} %b_hbm.1, bf16[64,256]{1,0:T(8,128)(2,1)} %filt_hbm.1, f32[256]{0:T(256)} %gain_hbm.1, bf16[256,256]{1,0:T(8,128)(2,1)} %wout_hbm.1), custom_call_target="tpu_custom_call" | custom-call | tf_op jit(solution)/shard_map/pallas_call | solution.py:239
  18.3 2.2 %convolution_convert_fusion = bf16[1024,256]{1,0:T(8,128)(2,1)} fusion(bf16[1024,256]{1,0:T(8,128)(2,1)} %shard_map.73, bf16[256,256]{1,0:T(8,128)(2,1)} %wout_hbm.1), kind=kOutput, calls=%fused_computation | convolution fusion | flops 134479872 | bytes 1179648 | tf_op jit(solution)/shard_map/dot_general | solution.py:283

commit v19 on v18

--- a/solution.py
+++ b/solution.py
@@ -11,7 +11,8 @@
 def layer_kernel(rows, span, pitch, x_hbm, w_hbm, k_hbm, b_hbm, filt_hbm, gain_hbm, wout_hbm,
                  out_ref, x_ref, w_ref, k_ref, b_ref, filt_ref, gain_ref, wout_ref, load_sem, pext,
                  shifted, kb, bb, send_col, recv_col, recv_row, stage, send_row,
-                 send_cor, recv_cor, ext, fb, qf, gated, send_sem, recv_sem):
+                 send_cor, recv_cor, ext, fb, qf, gated, edge_acc, halo_only, send_sem,
+                 recv_sem):
     width = out_ref.shape[1]
     wide = w_ref.shape[1]
     count = rows * span
@@ -193,6 +194,27 @@
     def _():
         product_copies[0].wait_send()
 
+    zero_row = jnp.zeros((1, wide), jnp.float32)
+    for i in range(rows + 2):
+        shifted[0, pl.ds(i * span, 1), :] = zero_row
+        shifted[2, pl.ds(i * span + span - 1, 1), :] = zero_row
+    halo_only[...] = jnp.zeros_like(halo_only)
+    sides = ((0, 0, 0), (span - 8, 1, 2))
+
+    def edge_partial(i, carry):
+        for k, (w0, side, tap) in enumerate(sides):
+            for grp in range(3):
+                lanes = pl.ds(grp * width, width)
+                acc = bb[0:8, lanes]
+                for a in range(3):
+                    src = pl.ds(pl.multiple_of((i + a) * span, 8) + w0, 8)
+                    for b in range(3):
+                        acc = acc + shifted[b, src, lanes] * kb[a * 3 + b, 0:8, lanes]
+                edge_acc[i, pl.ds(8 * k, 8), lanes] = acc
+        return carry
+
+    lax.fori_loop(0, rows, edge_partial, 0)
+
     for cp, cond in zip(copies[:4], send_when[:4]):
         guarded(cond, cp.wait_send)
     for cp, cond in zip(copies[:4], recv_when[:4]):
@@ -200,12 +222,27 @@
     stage[0] = recv_col[0].astype(jnp.float32)
     stage[1] = recv_col[1].astype(jnp.float32)
     for i in range(rows):
-        shifted[0, pl.ds((1 + i) * span, 1), :] = stage[0, i : i + 1, :]
-        shifted[2, pl.ds((1 + i) * span + span - 1, 1), :] = stage[1, i : i + 1, :]
-    halo_at = pl.multiple_of(partner * (rows + 1) * span, 8)
-    shifted[0, pl.ds(halo_at, 1), :] = recv_cor[0, 0:1, :].astype(jnp.float32)
-    shifted[2, pl.ds(halo_at + span - 1, 1), :] = recv_cor[1, 0:1, :].astype(jnp.float32)
-    lax.fori_loop(0, rows, outer_body, 0)
+        halo_only[0, 1 + i, 0:1, :] = stage[0, i : i + 1, :]
+        halo_only[1, 1 + i, 7:8, :] = stage[1, i : i + 1, :]
+    halo_row = partner * (rows + 1)
+    halo_only[0, halo_row, 0:1, :] = recv_cor[0, 0:1, :].astype(jnp.float32)
+    halo_only[1, halo_row, 7:8, :] = recv_cor[1, 0:1, :].astype(jnp.float32)
+
+    def edge_final(i, carry):
+        for k, (w0, side, tap) in enumerate(sides):
+            res = []
+            for grp in range(3):
+                lanes = pl.ds(grp * width, width)
+                acc = edge_acc[i, pl.ds(8 * k, 8), lanes]
+                for a in range(3):
+                    acc = acc + halo_only[side, i + a, :, lanes] * kb[a * 3 + tap, 0:8, lanes]
+                res.append(acc.astype(jnp.bfloat16).astype(jnp.float32))
+            qf[pl.ds(pl.multiple_of(i * span, 8) + w0, 8), :] = res[0]
+            ext[rows + i, pl.ds(w0, 8), :] = (
+                (res[1] * res[2]).astype(jnp.bfloat16).astype(jnp.float32))
+        return carry
+
+    lax.fori_loop(0, rows, edge_final, 0)
 
     @pl.when(r == 0)
     def _():
@@ -265,6 +302,8 @@
             pltpu.VMEM((2 * row_count, 8, width), jnp.float32),
             pltpu.VMEM((flat, width), jnp.float32),
             pltpu.VMEM((flat, width), jnp.float32),
+            pltpu.VMEM((row_count, 16, wide), jnp.float32),
+            pltpu.VMEM((2, row_count + 2, 8, wide), jnp.float32),
             pltpu.SemaphoreType.DMA((8,)),
             pltpu.SemaphoreType.DMA((8,)),
         ],

time: 20.6 us -> 21.4 us (1.039)
  Pallas kernels: 18.3 us -> 19.1 us
    pallas_call x1, Pallas kernels: 18.3 us -> 19.1 us  [on_device(): pl.pallas_call(functools.partial(layer_kernel, row_count, col_count, pitc...]
where the time goes in v19:
time: 21.4 us; the launch traced here: 21.2 us
  Pallas kernels  19.1 us (89%)
  matrix products  2.16 us (10%)
    pallas_call x1, Pallas kernels, on_device(): pl.pallas_call(functools.partial(layer_kernel, row_count, col_count, pitc...  19.1 us
    dot_general x1, matrix products, on_device(): jnp.dot(out, w_out, preferred_element_type=jnp.float32).astype(jnp.bfloat16)  2.16 us

profile of v19, /device:TPU:161, one launch (start us, length us, event | category | flops | bytes accessed | tf_op | source)
XLA Modules:
  0.0 21.2 jit_solution(7678578386581148490)
XLA Ops:
  0.0 19.1 %shard_map.73 = bf16[1024,256]{1,0:T(8,128)(2,1)} custom-call(bf16[1024,256]{1,0:T(8,128)(2,1)} %bitcast.4, bf16[256,768]{1,0:T(8,128)(2,1)} %w_hbm.1, bf16[3,3,768]{2,1,0:T(4,128)(2,1)} %k_hbm.1, f32[768]{0:T(1024)} %b_hbm.1, bf16[64,256]{1,0:T(8,128)(2,1)} %filt_hbm.1, f32[256]{0:T(256)} %gain_hbm.1, bf16[256,256]{1,0:T(8,128)(2,1)} %wout_hbm.1), custom_call_target="tpu_custom_call" | custom-call | tf_op jit(solution)/shard_map/pallas_call | solution.py:276
  19.1 2.2 %convolution_convert_fusion = bf16[1024,256]{1,0:T(8,128)(2,1)} fusion(bf16[1024,256]{1,0:T(8,128)(2,1)} %shard_map.73, bf16[256,256]{1,0:T(8,128)(2,1)} %wout_hbm.1), kind=kOutput, calls=%fused_computation | convolution fusion | flops 134479872 | bytes 1179648 | tf_op jit(solution)/shard_map/dot_general | solution.py:322
